TPU v7x, 32 devices: a whole 2x2x4 slice. The times are simulated.
32 devices in a mesh: groups: 1, ctx: 2 (over x), fsdp: 16 (over z, y, core).
Axes of the slice: x: 2, y: 2, z: 4, core: 2. Of those that a mesh axis runs over, the one named last changes fastest.
Arguments:
- tokens: bfloat16 [16, 256, 3072], P(('groups', 'fsdp'), 'ctx'), may hold values from -600 to 600
- trace_index: int32 [16, 256], P(('groups', 'fsdp'), 'ctx'), may hold values from 0 to 1, never falling along the last dimension, each value on 1 to 192 neighbouring positions
- input_norm_scale: bfloat16 [3072], replicated, may hold values from 0.099609375 to 1.8984375
- query_weight: bfloat16 [3072, 2048], P('fsdp'), may hold values from -0.109375 to 0.109375
- key_weight: bfloat16 [3072, 1024], P('fsdp'), may hold values from -0.109375 to 0.109375
- value_weight: bfloat16 [3072, 1024], P('fsdp'), may hold values from -0.109375 to 0.109375
- query_down_weight: bfloat16 [3072, 16], replicated, may hold values from -0.109375 to 0.109375
- query_up_weight: bfloat16 [16, 2048], replicated, may hold values from -1.5 to 1.5
- value_down_weight: bfloat16 [3072, 16], replicated, may hold values from -0.109375 to 0.109375
- value_up_weight: bfloat16 [16, 1024], replicated, may hold values from -1.5 to 1.5
- output_gradient: bfloat16 [16, 256, 2048], P(('groups', 'fsdp'), 'ctx'), may hold values from -24 to 24
Outputs:
- grad_a_query: float32 [3072, 16], P('groups')
- grad_b_query: float32 [16, 2048], P('groups')
- grad_a_value: float32 [3072, 16], P('groups')
- grad_b_value: float32 [16, 1024], P('groups')
Inputs may be any that keep to these rules, and one draw needn't show every extreme that they name: `trace_index`: ids never fall along a sequence; one trace holds at most 192 positions.
All inputs are finite; a program needn't handle non-finite values.
Results may differ from a plain program's by a relative error of at most 0.013.
Values may be sent and summed in bfloat16 or wider, within the bound.
A program may use at most 128 MiB of HBM per device.

v0:
```python
import functools
import math

import jax
import jax.numpy as jnp
from jax import lax
from jax.experimental import pallas as pl
from jax.experimental.pallas import tpu as pltpu
from jax.sharding import PartitionSpec as P

HEAD_SIZE = 128


CAP = 50.0
QSCALE = 1.0 / 12.0
ADAPTER_NAME = 0.5
EPS = 1e-06


def shifted(value, axis, by):
    devices = lax.axis_size(axis)
    pairs = [(i, i + by) for i in range(devices) if 0 <= i + by < devices]
    return lax.ppermute(value, axis, pairs)


def normed_rows(values, gain):
    flt = values.astype(jnp.float32)
    meansq = jnp.mean(flt * flt, axis=-1, keepdims=True)
    return (flt * lax.rsqrt(meansq + EPS) * gain.astype(jnp.float32)).astype(jnp.bfloat16)


def add_rows(left, piece):
    return jnp.dot(left, piece, preferred_element_type=jnp.float32)


def attend_head(operands, mask):
    q_head, k_head, v_head, g_head = operands
    s = jnp.einsum("igd,jd->gij", q_head, k_head, preferred_element_type=jnp.float32) * QSCALE
    t = jnp.tanh(s / CAP)
    capped = CAP * t
    expo = jnp.where(mask[None], jnp.exp(capped), jnp.float32(0.0))
    weights = expo / jnp.sum(expo, axis=-1, keepdims=True)
    weights16 = weights.astype(jnp.bfloat16)
    attended = jnp.einsum("gij,jd->igd", weights16, v_head, preferred_element_type=jnp.float32)
    dweight = jnp.einsum("igd,jd->gij", g_head, v_head, preferred_element_type=jnp.float32)
    delta = jnp.sum(g_head.astype(jnp.float32) * attended, axis=-1).T
    dscore = (weights * (dweight - delta[..., None]) * (1.0 - t * t) * QSCALE).astype(jnp.bfloat16)
    query_gradient = jnp.einsum(
        "gij,jd->igd", dscore, k_head, preferred_element_type=jnp.float32
    ).astype(jnp.bfloat16)
    value_gradient = jnp.einsum(
        "gij,igd->jd", weights16, g_head, preferred_element_type=jnp.float32
    )
    return (query_gradient, value_gradient)


def partial_attend(mask):

    def run_head(operands):
        return attend_head(operands, mask)

    return run_head


def on_device(
    tokens,
    trace_index,
    input_norm_scale,
    query_weight,
    key_weight,
    value_weight,
    query_down_weight,
    query_up_weight,
    value_down_weight,
    value_up_weight,
    output_gradient,
):
    window_width = tokens.shape[1]
    feats = tokens.shape[2]
    heads_kv = key_weight.shape[1] // HEAD_SIZE
    heads_q = query_weight.shape[1] // HEAD_SIZE
    head_group = heads_q // heads_kv
    normalized_input = normed_rows(tokens.reshape(window_width, feats), input_norm_scale)
    seg_own = trace_index.reshape(window_width).astype(jnp.bfloat16)
    seg_parts = []

    def add_keyval(piece):
        return add_rows(normalized_input, piece)

    query_frozen = add_rows(
        normalized_input, lax.all_gather(query_weight, "fsdp", axis=0, tiled=True)
    )
    k_base = add_keyval(lax.all_gather(key_weight, "fsdp", axis=0, tiled=True))
    value_frozen = add_keyval(lax.all_gather(value_weight, "fsdp", axis=0, tiled=True))
    query_reduced = jnp.dot(
        normalized_input, query_down_weight, preferred_element_type=jnp.float32
    ).astype(jnp.bfloat16)
    reduced_rows = jnp.dot(
        normalized_input, value_down_weight, preferred_element_type=jnp.float32
    ).astype(jnp.bfloat16)
    query_matrix = (
        query_frozen
        + ADAPTER_NAME * jnp.dot(query_reduced, query_up_weight, preferred_element_type=jnp.float32)
    ).astype(jnp.bfloat16)
    key_rows = k_base.astype(jnp.bfloat16)
    value_rows = (
        value_frozen
        + ADAPTER_NAME * jnp.dot(reduced_rows, value_up_weight, preferred_element_type=jnp.float32)
    ).astype(jnp.bfloat16)
    key_parts = []
    value_parts = []
    for distance in (2, 1):
        key_prev, value_prev, seg_prev = shifted((key_rows, value_rows, seg_own), "ctx", distance)
        key_parts.append(key_prev)
        value_parts.append(value_prev)
        seg_parts.append(seg_prev)
    keys_all = jnp.concatenate(key_parts + [key_rows], 0)
    values_all = jnp.concatenate(value_parts + [value_rows], 0)
    seg_keys = jnp.concatenate(seg_parts + [seg_own], 0)
    pos_q = jnp.arange(window_width, dtype=jnp.int32)[:, None]
    pos_k = jnp.arange(3 * window_width, dtype=jnp.int32)[None, :]
    position = lax.axis_index("ctx")
    mask = (
        (pos_k > pos_q)
        & (pos_k <= pos_q + 2 * window_width)
        & (seg_keys[None, :] == seg_own[:, None])
    )
    mask = mask & (
        (pos_k >= 2 * window_width) | (pos_k >= window_width) & (position >= 1) | (position >= 2)
    )
    q_heads = jnp.moveaxis(
        query_matrix.reshape(window_width, heads_kv, head_group, HEAD_SIZE), 1, 0
    )
    g_heads = jnp.moveaxis(
        output_gradient.reshape(window_width, heads_kv, head_group, HEAD_SIZE), 1, 0
    )
    k_heads = jnp.moveaxis(keys_all.reshape(3 * window_width, heads_kv, HEAD_SIZE), 1, 0)
    v_heads = jnp.moveaxis(values_all.reshape(3 * window_width, heads_kv, HEAD_SIZE), 1, 0)
    dquery_heads, dvalue_heads = lax.map(partial_attend(mask), (q_heads, k_heads, v_heads, g_heads))
    query_gradient = jnp.moveaxis(dquery_heads, 0, 1).reshape(window_width, heads_q * HEAD_SIZE)
    dvalue_triple = jnp.moveaxis(dvalue_heads, 0, 1).reshape(3 * window_width, heads_kv * HEAD_SIZE)
    value_gradient = dvalue_triple[2 * window_width :]
    for distance in (1, 2):
        begin = (2 - distance) * window_width
        value_gradient = value_gradient + shifted(
            dvalue_triple[begin : begin + window_width], "ctx", -distance
        )
    query_backward = jnp.dot(
        query_gradient, query_up_weight.T, preferred_element_type=jnp.float32
    ).astype(jnp.bfloat16)
    value_backward = jnp.dot(
        value_gradient, value_up_weight.astype(jnp.float32).T, precision=lax.Precision.HIGHEST
    )
    part_aq = jnp.dot(normalized_input.T, query_backward, preferred_element_type=jnp.float32)
    part_bq = jnp.dot(query_reduced.T, query_gradient, preferred_element_type=jnp.float32)
    part_av = jnp.dot(
        normalized_input.astype(jnp.float32).T, value_backward, precision=lax.Precision.HIGHEST
    )
    part_bv = jnp.dot(
        reduced_rows.astype(jnp.float32).T, value_gradient, precision=lax.Precision.HIGHEST
    )
    sum_aq, sum_bq, sum_av, sum_bv = lax.psum((part_aq, part_bq, part_av, part_bv), ("ctx", "fsdp"))
    token_total = lax.axis_size("ctx") * lax.axis_size("fsdp") * window_width
    coefficient = ADAPTER_NAME / math.sqrt(token_total)
    return (sum_aq * coefficient, sum_bq * coefficient, sum_av * coefficient, sum_bv * coefficient)


F32 = jnp.float32
BF16 = jnp.bfloat16
PLANE = 8


def dot(a, b, dims=((1,), (0,))):
    return lax.dot_general(a, b, (dims, ((), ())), preferred_element_type=F32)


def plane_kernel(
    chain, coefficient,
    raw, seg, gain, wq, wk, wv, qd, qu, vd, vu, grad,
    OUT,
    N, M, W, G, SG, acc, DQ, DV, LQ, LV, A, RA, RS, T,
    local_sem, w_send, w_recv, t_send, t_recv, g_send, g_recv, s_send, s_recv,
    up_send, up_recv, down_send, down_recv,
    r1_send, r1_recv, r2_send, r2_recv, r3_send, r3_recv,
):
    x = lax.axis_index("ctx")
    f = lax.axis_index("fsdp")
    z = f // 4
    y = (f // 2) % 2
    c = f % 2
    tok, feats = raw.shape
    rows = wq.shape[0]
    qcols = wq.shape[1] // PLANE
    kcols = wk.shape[1] // PLANE
    piece = feats // PLANE
    plane_rows = 4 * rows
    seq = 2 * tok

    def coords(r):
        px = 1 - x if r & 4 else x
        py = 1 - y if r & 2 else y
        pc = 1 - c if r & 1 else c
        return px, py, pc

    def head_of(r):
        px, py, pc = coords(r)
        return (px * 2 + py) * 2 + pc

    def peer(r):
        px, py, pc = coords(r)
        return {"ctx": px, "fsdp": (z * 2 + py) * 2 + pc}

    def above(pz):
        return {"ctx": x, "fsdp": (pz * 2 + y) * 2 + c}

    def tok_rows(r):
        px, py, pc = coords(r)
        return pl.ds(pl.multiple_of(((py * 2 + pc) * 2 + px) * tok, tok), tok)

    def tok_slot(r):
        px, py, pc = coords(r)
        return (py * 2 + pc) * 2 + px

    def tok_piece(r, part):
        px, py, pc = coords(r)
        if part is None:
            return tok_rows(r)
        begin = ((py * 2 + pc) * 2 + px) * tok + part * (tok // 2)
        return pl.ds(pl.multiple_of(begin, tok // 2), tok // 2)

    def remote(src, dst, send, recv, device):
        return pltpu.make_async_remote_copy(
            src_ref=src, dst_ref=dst, send_sem=send, recv_sem=recv,
            device_id=device, device_id_type=pl.DeviceIdType.MESH,
        )

    barrier = pltpu.get_barrier_semaphore()
    for r in range(1, PLANE):
        pl.semaphore_signal(barrier, inc=1, device_id=peer(r), device_id_type=pl.DeviceIdType.MESH)
    for d in range(1, chain):
        pl.semaphore_signal(
            barrier, inc=1, device_id=above((z + d) % chain), device_id_type=pl.DeviceIdType.MESH
        )

    def w_rows(r):
        px, py, pc = coords(r)
        return pl.ds(pl.multiple_of(((z * 2 + py) * 2 + pc) * rows, rows), rows)

    def w_parts(r):
        h = head_of(r)
        own = w_rows(0)
        return (
            (wq.at[:, pl.ds(pl.multiple_of(h * qcols, qcols), qcols)], W.at[own, pl.ds(0, qcols)]),
            (wk.at[:, pl.ds(pl.multiple_of(h * kcols, kcols), kcols)], W.at[own, pl.ds(qcols, kcols)]),
            (wv.at[:, pl.ds(pl.multiple_of(h * kcols, kcols), kcols)], W.at[own, pl.ds(qcols + kcols, kcols)]),
        )

    def g_cols(r):
        h = head_of(r)
        return grad.at[:, pl.ds(pl.multiple_of(h * qcols, qcols), qcols)]

    local = [pltpu.make_async_copy(a, b, local_sem.at[i]) for i, (a, b) in enumerate(w_parts(0))]
    local.append(pltpu.make_async_copy(raw, N.at[tok_rows(0)], local_sem.at[3]))
    local.append(pltpu.make_async_copy(g_cols(0), G.at[tok_rows(0)], local_sem.at[4]))
    local.append(pltpu.make_async_copy(seg, SG.at[tok_slot(0)], local_sem.at[5]))
    for copy in local:
        copy.start()
    pl.semaphore_wait(barrier, PLANE - 1 + chain - 1)

    w_copies = {}
    for r in (1, 2, 3):
        w_copies[r] = [
            remote(a, b, w_send.at[r, i], w_recv.at[r, i], peer(r)) for i, (a, b) in enumerate(w_parts(r))
        ]
        for copy in w_copies[r]:
            copy.start()
    t_copies = []

    def send_token(r_mine, r_there, hop, part=None):
        at = N.at[tok_piece(r_mine, part)]
        source = at
        if r_mine == 0:
            source = raw if part is None else raw.at[pl.ds(part * (tok // 2), tok // 2)]
        i = part or 0
        copy = remote(source, at, t_send.at[r_there, i], t_recv.at[r_there, i], peer(hop))
        copy.start()
        t_copies.append(copy)

    send_token(0, 2, 2, 0)
    send_token(0, 2, 2, 1)
    send_token(0, 4, 4)
    send_token(0, 1, 1)
    g_copies = {}
    s_copies = {}
    for r in range(1, PLANE):
        g_copies[r] = remote(g_cols(r), G.at[tok_rows(0)], g_send.at[r], g_recv.at[r], peer(r))
        s_copies[r] = remote(seg, SG.at[tok_slot(0)], s_send.at[r], s_recv.at[r], peer(r))

    def half_rows(plane, half):
        py = y if half == 0 else 1 - y
        return pl.ds(pl.multiple_of((plane * 4 + py * 2) * rows, 2 * rows), 2 * rows)

    def up_copy(t, half):
        at = W.at[half_rows(z - t, half)]
        return remote(at, at, up_send.at[t, half], up_recv.at[t, half], above(z + 1))

    def down_copy(t, half):
        at = W.at[half_rows(z + t, half)]
        return remote(at, at, down_send.at[t, half], down_recv.at[t, half], above(z - 1))

    def up_arrival(t, half):
        at = W.at[half_rows(z - 1 - t, half)]
        return remote(at, at, up_send.at[t, half], up_recv.at[t, half], above(z - 1))

    def down_arrival(t, half):
        at = W.at[half_rows(z + 1 + t, half)]
        return remote(at, at, down_send.at[t, half], down_recv.at[t, half], above(z + 1))

    def has_up(t):
        return (z < chain - 1) & (z - t >= 0)

    def has_down(t):
        return (z > 0) & (z + t <= chain - 1)

    def send_chain(t, half):
        @pl.when(has_up(t))
        def _():
            up_copy(t, half).start()

        @pl.when(has_down(t))
        def _():
            down_copy(t, half).start()

    def recv_chain(t, half):
        @pl.when(z - 1 - t >= 0)
        def _():
            up_arrival(t, half).wait_recv()

        @pl.when(z + 1 + t <= chain - 1)
        def _():
            down_arrival(t, half).wait_recv()

    def wait_token(r, part=None):
        at = N.at[tok_piece(r, part)]
        i = part or 0
        remote(at, at, t_send.at[r, i], t_recv.at[r, i], peer(1)).wait_recv()

    def wait_weight(r):
        at = w_rows(r)
        for i, (lo, width) in enumerate(((0, qcols), (qcols, kcols), (qcols + kcols, kcols))):
            ref = W.at[at, pl.ds(lo, width)]
            remote(ref, ref, w_send.at[r, i], w_recv.at[r, i], peer(r)).wait_recv()

    part_rows = 4 * tok

    def part_at(part, i, height):
        py = y if part == 0 else 1 - y
        return pl.ds(pl.multiple_of(py * part_rows + i * height, height), height)

    def prepare(r):
        height = tok // 2

        @pl.loop(0, 2)
        def _(i):
            px, py, pc = coords(r)
            begin = ((py * 2 + pc) * 2 + px) * tok + i * height
            at = pl.ds(pl.multiple_of(begin, height), height)
            flt = N[at, :].astype(F32)
            meansq = jnp.sum(flt * flt, axis=-1, keepdims=True) / feats
            M[at, :] = (flt * lax.rsqrt(meansq + EPS) * gain[...].astype(F32).reshape(1, feats)).astype(BF16)

        at = tok_rows(r)
        block = M[at, :]
        LQ[at, :] = dot(block, qd[...], ((1,), (1,))).astype(BF16)
        LV[at, :] = dot(block, vd[...], ((1,), (1,))).astype(BF16)

    def add_piece(plane, half, part, first=False):
        chosen = half_rows(plane, half)

        @pl.loop(0, part_rows // seq)
        def _(i):
            at = part_at(part, i, seq)
            value = dot(M[at, chosen], W[chosen, :])
            acc[at, :] = value if first else acc[at, :] + value

    def add_step(t, half, part):
        @pl.when(z - 1 - t >= 0)
        def _():
            add_piece(z - 1 - t, half, part)

        @pl.when(z + 1 + t <= chain - 1)
        def _():
            add_piece(z + 1 + t, half, part)

    for i in range(3):
        local[i].wait()
    wait_weight(1)
    send_chain(0, 0)
    wait_weight(2)
    wait_weight(3)
    send_chain(0, 1)
    for r in range(1, PLANE):
        s_copies[r].start()
    recv_chain(0, 0)
    send_chain(1, 0)
    local[3].wait()
    prepare(0)
    wait_token(1)
    prepare(1)
    wait_token(4)
    send_token(4, 5, 1)
    wait_token(2, 0)
    send_token(2, 6, 4, 0)
    recv_chain(0, 1)
    send_chain(1, 1)
    prepare(4)
    wait_token(5)
    prepare(5)
    wait_token(2, 1)
    send_token(2, 6, 4, 1)
    send_token(2, 3, 1)
    for r in range(1, PLANE):
        g_copies[r].start()
    prepare(2)
    add_piece(z, 0, 0, True)
    add_piece(z, 1, 0)
    for half in range(2):
        add_step(0, half, 0)
    wait_token(3)
    prepare(3)
    for t in range(1, chain - 2):
        for half in range(2):
            recv_chain(t, half)
            send_chain(t + 1, half)
            add_step(t, half, 0)
    wait_token(6, 0)
    wait_token(6, 1)
    send_token(6, 7, 1)
    prepare(6)
    wait_token(7)
    prepare(7)
    add_piece(z, 0, 1, True)
    add_piece(z, 1, 1)
    for t in range(chain - 2):
        for half in range(2):
            add_step(t, half, 1)
    for half in range(2):
        recv_chain(chain - 2, half)
        for part in range(2):
            add_step(chain - 2, half, part)

    tiles = PLANE * tok // seq
    h = head_of(0)
    qu_own = qu[:, pl.ds(pl.multiple_of(h * qcols, qcols), qcols)]
    vu_own = vu[:, pl.ds(pl.multiple_of(h * kcols, kcols), kcols)]
    local[4].wait()
    local[5].wait()
    for r in range(1, PLANE):
        at = G.at[tok_rows(r)]
        remote(at, at, g_send.at[r], g_recv.at[r], peer(r)).wait_recv()
        at = SG.at[tok_slot(r)]
        remote(at, at, s_send.at[r], s_recv.at[r], peer(r)).wait_recv()

    pos_i = lax.broadcasted_iota(jnp.int32, (seq, seq), 0)
    pos_j = lax.broadcasted_iota(jnp.int32, (seq, seq), 1)
    band = (pos_j <= pos_i) & (pos_j > pos_i - 2 * tok)

    @pl.loop(0, tiles, unroll=2)
    def _(i):
        at = pl.ds(pl.multiple_of(i * seq, seq), seq)
        q_all = (acc[at, 0:qcols] + ADAPTER_NAME * dot(LQ[at, :], qu_own)).astype(BF16)
        k = acc[at, qcols:qcols + kcols].astype(BF16)
        v = (acc[at, qcols + kcols:] + ADAPTER_NAME * dot(LV[at, :], vu_own)).astype(BF16)
        g_all = G[at, :]
        traces = [SG[2 * i].astype(F32), SG[2 * i + 1].astype(F32)]
        along = jnp.concatenate(traces, axis=1)
        turned = [jnp.broadcast_to(own, (tok, tok)).T for own in traces]
        across = jnp.concatenate([jnp.concatenate([own, own], axis=1) for own in turned], axis=0)
        mask = band & (across == along)
        dv = jnp.zeros((seq, kcols), F32)
        for n in range(qcols // kcols):
            q = q_all[:, n * kcols:(n + 1) * kcols]
            g = g_all[:, n * kcols:(n + 1) * kcols]
            t = jnp.tanh(dot(q, k, ((1,), (1,))) * (QSCALE / CAP))
            expo = jnp.where(mask, jnp.exp(CAP * t), 0.0)
            weights = expo * (1.0 / jnp.sum(expo, axis=-1, keepdims=True))
            weights16 = weights.astype(BF16)
            attended = dot(weights16, v)
            dweight = dot(g, v, ((1,), (1,)))
            delta = jnp.sum(g.astype(F32) * attended, axis=-1, keepdims=True)
            dscore = (weights * (dweight - delta) * (1.0 - t * t)).astype(BF16)
            DQ[at, n * kcols:(n + 1) * kcols] = (dot(dscore, k) * QSCALE).astype(BF16)
            dv = dv + dot(weights16, g, ((0,), (0,)))
        DV[at, :] = dv.astype(BF16)

    pull_q = dot(qu_own, DQ[...], ((1,), (1,))).astype(BF16)
    pull_v = dot(vu_own, DV[...], ((1,), (1,))).astype(BF16)
    pull = jnp.concatenate([pull_q, pull_v], axis=0)
    ranks = pull.shape[0]
    half_rank = ranks // 2
    r1_copies = []
    for r in (7, 6, 5, 4, 3, 2, 1, 0):
        columns = pl.ds(pl.multiple_of(head_of(r) * piece, piece), piece)
        A[r] = dot(pull, M[:, columns]).astype(BF16)
        if r > 0:
            copy = remote(A.at[r], RA.at[r], r1_send.at[r], r1_recv.at[r], peer(r))
            copy.start()
            r1_copies.append(copy)
    own_sum = RS.at[z]
    own_sum[ranks:, 0:qcols] = dot(LQ[...], DQ[...], ((0,), (0,))).astype(BF16)
    own_sum[ranks:, qcols:qcols + kcols] = dot(LV[...], DV[...], ((0,), (0,))).astype(BF16)
    for copy in r1_copies:
        copy.wait_recv()
    total = A[0].astype(F32)
    for r in range(1, PLANE):
        total = total + RA[r].astype(F32)
    own_sum[0:ranks, :] = total.astype(BF16)
    r2_copies = []
    for d in range(1, chain):
        copy = remote(own_sum, own_sum, r2_send.at[d], r2_recv.at[d], above((z + d) % chain))
        copy.start()
        r2_copies.append(copy)
    for d in range(1, chain):
        at = RS.at[(z - d + chain) % chain]
        remote(at, at, r2_send.at[d], r2_recv.at[d], above((z + d) % chain)).wait_recv()
    total = RS[0].astype(F32)
    for d in range(1, chain):
        total = total + RS[d].astype(F32)
    total = (total * coefficient).astype(BF16)
    T[...] = total
    r3_copies = []
    for r in (7, 6, 5, 4, 3, 2, 1):
        copy = remote(T, OUT.at[h], r3_send.at[r], r3_recv.at[r], peer(r))
        copy.start()
        r3_copies.append(copy)
    OUT[h] = total
    for r in range(1, PLANE):
        at = OUT.at[head_of(r)]
        remote(at, at, r3_send.at[r], r3_recv.at[r], peer(r)).wait_recv()

    for r in (1, 2, 3):
        for copy in w_copies[r]:
            copy.wait_send()
    for copy in t_copies:
        copy.wait_send()
    for r in range(1, PLANE):
        g_copies[r].wait_send()
        s_copies[r].wait_send()
    for t in range(chain - 1):
        for half in range(2):
            @pl.when(has_up(t))
            def _():
                up_copy(t, half).wait_send()

            @pl.when(has_down(t))
            def _():
                down_copy(t, half).wait_send()
    for copy in r1_copies + r2_copies + r3_copies:
        copy.wait_send()


def unpack_kernel(gathered, out_aq, out_bq, out_av, out_bv):
    ranks, feats = out_aq.shape
    piece = feats // PLANE
    qcols = out_bq.shape[1] // PLANE
    kcols = out_bv.shape[1] // PLANE
    for h in range(PLANE):
        value = gathered[h].astype(F32)
        out_aq[:, h * piece:(h + 1) * piece] = value[0:ranks]
        out_av[:, h * piece:(h + 1) * piece] = value[ranks:2 * ranks]
        out_bq[:, h * qcols:(h + 1) * qcols] = value[2 * ranks:, 0:qcols]
        out_bv[:, h * kcols:(h + 1) * kcols] = value[2 * ranks:, qcols:qcols + kcols]


def on_plane(
    tokens,
    trace_index,
    input_norm_scale,
    query_weight,
    key_weight,
    value_weight,
    query_down_weight,
    query_up_weight,
    value_down_weight,
    value_up_weight,
    output_gradient,
):
    tok = tokens.shape[1]
    feats = tokens.shape[2]
    fsdp = lax.axis_size("fsdp")
    chain = fsdp // 4
    ranks = query_down_weight.shape[1]
    qcols = query_weight.shape[1] // PLANE
    kcols = key_weight.shape[1] // PLANE
    columns = qcols + 2 * kcols
    piece = feats // PLANE
    many = PLANE * tok
    token_total = lax.axis_size("ctx") * fsdp * tok
    coefficient = ADAPTER_NAME / math.sqrt(token_total)
    hbm = pl.BlockSpec(memory_space=pl.ANY)
    vmem = pl.BlockSpec(memory_space=pltpu.VMEM)
    dma = pltpu.SemaphoreType.DMA
    steps = max(chain - 1, 1)
    gathered = pl.pallas_call(
        functools.partial(plane_kernel, chain, coefficient),
        out_shape=jax.ShapeDtypeStruct((PLANE, 3 * ranks, piece), BF16),
        in_specs=[hbm, hbm, vmem, hbm, hbm, hbm, vmem, vmem, vmem, vmem, hbm],
        out_specs=vmem,
        scratch_shapes=[
            pltpu.VMEM((many, feats), BF16),
            pltpu.VMEM((many, feats), BF16),
            pltpu.VMEM((feats, columns), BF16),
            pltpu.VMEM((many, qcols), BF16),
            pltpu.VMEM((PLANE, 1, tok), jnp.int32),
            pltpu.VMEM((many, columns), F32),
            pltpu.VMEM((many, qcols), BF16),
            pltpu.VMEM((many, kcols), BF16),
            pltpu.VMEM((many, ranks), BF16),
            pltpu.VMEM((many, ranks), BF16),
            pltpu.VMEM((PLANE, 2 * ranks, piece), BF16),
            pltpu.VMEM((PLANE, 2 * ranks, piece), BF16),
            pltpu.VMEM((chain, 3 * ranks, piece), BF16),
            pltpu.VMEM((3 * ranks, piece), BF16),
            dma((6,)),
            dma((4, 3)), dma((4, 3)),
            dma((8, 2)), dma((8, 2)), dma((8,)), dma((8,)), dma((8,)), dma((8,)),
            dma((steps, 2)), dma((steps, 2)), dma((steps, 2)), dma((steps, 2)),
            dma((8,)), dma((8,)), dma((max(chain, 2),)), dma((max(chain, 2),)), dma((8,)), dma((8,)),
        ],
        compiler_params=pltpu.CompilerParams(
            collective_id=0, has_side_effects=True, vmem_limit_bytes=56 * 1024 * 1024
        ),
    )(
        tokens.reshape(tok, feats), trace_index, input_norm_scale,
        query_weight, key_weight, value_weight,
        query_down_weight.T, query_up_weight, value_down_weight.T, value_up_weight,
        output_gradient.reshape(tok, output_gradient.shape[2]),
    )
    aq, bq, av, bv = pl.pallas_call(
        unpack_kernel,
        out_shape=(
            jax.ShapeDtypeStruct((ranks, feats), F32),
            jax.ShapeDtypeStruct((ranks, query_weight.shape[1]), F32),
            jax.ShapeDtypeStruct((ranks, feats), F32),
            jax.ShapeDtypeStruct((ranks, value_weight.shape[1]), F32),
        ),
        in_specs=[vmem],
        out_specs=(vmem, vmem, vmem, vmem),
    )(gathered)
    return (aq.T, bq, av.T, bv)


def solution(mesh):
    shape = mesh.shape
    planes = shape["groups"] == 1 and shape["ctx"] == 2 and shape["fsdp"] % 4 == 0 and shape["fsdp"] > 8
    return jax.shard_map(
        on_plane if planes else on_device,
        mesh=mesh,
        in_specs=(
            P(("groups", "fsdp"), "ctx", None),
            P(("groups", "fsdp"), "ctx"),
            P(),
            P("fsdp", None),
            P("fsdp", None),
            P("fsdp", None),
            P(),
            P(),
            P(),
            P(),
            P(("groups", "fsdp"), "ctx", None),
        ),
        out_specs=(P("groups", None), P("groups", None), P("groups", None), P("groups", None)),
        check_vma=False,
    )
```

profile of v0, /device:TPU:0, one launch (start us, length us, event | category | flops | bytes accessed | tf_op | source)
XLA Modules:
  0.0 84.2 jit_solution(10877078190160230012)
XLA Ops:
  0.6 81.8 %shard_map.138.gathered = bf16[8,48,384]{2,1,0:T(8,128)(2,1)} custom-call(bf16[128,3072]{1,0:T(8,128)(2,1)} %bitcast.6, s32[1,128]{1,0:T(1,128)} %seg.1, bf16[3072]{0:T(1024)(128)(2,1)} %gain.1, bf16[192,2048]{1,0:T(8,128)(2,1)} %wq.1, bf16[192,1024]{1,0:T(8,128)(2,1)} %wk.1, bf16[192,1024]{1,0:T(8,128)(2,1)} %wv.1, bf16[16,3072]{1,0:T(8,128)(2,1)} %bitcast.8, ...), custom_call_target="tpu_custom_call" | custom-call | tf_op jit(solution)/shard_map/pallas_call | solution.py:604
  82.5 1.8 %shard_map.139 = (f32[16,3072]{1,0:T(8,128)}, f32[16,2048]{1,0:T(8,128)}, f32[16,3072]{1,0:T(8,128)}, f32[16,1024]{1,0:T(8,128)}) custom-call(bf16[8,48,384]{2,1,0:T(8,128)(2,1)} %shard_map.138.gathered), custom_call_target="tpu_custom_call" | custom-call | tf_op jit(solution)/shard_map/pallas_call | solution.py:639
where the time goes:
time: 84.4 us; the launch traced here: 84.2 us
  Pallas kernels  83.6 us (99%)
    pallas_call x1, Pallas kernels, on_plane(): pl.pallas_call(functools.partial(plane_kernel, chain, coefficient), out_s...  81.8 us
    pallas_call x1, Pallas kernels, on_plane(): pl.pallas_call(unpack_kernel, out_shape=(jax.ShapeDtypeStruct((ranks, fea...  1.78 us

commit v1 on v0

--- a/solution.py
+++ b/solution.py
@@ -177,11 +177,13 @@
 def plane_kernel(
     chain, coefficient,
     raw, seg, gain, wq, wk, wv, qd, qu, vd, vu, grad,
-    OUT,
-    N, M, W, G, SG, acc, DQ, DV, LQ, LV, A, RA, RS, T,
+    OUTQ, OUTV,
+    N, M, WA, WV, G, SG, acc, accv, P, C, K, DQ, DV, LQ, LV,
+    AQ, RAQ, RSQ, TQ, AV, RAV, RSV, TV,
     local_sem, w_send, w_recv, t_send, t_recv, g_send, g_recv, s_send, s_recv,
-    up_send, up_recv, down_send, down_recv,
-    r1_send, r1_recv, r2_send, r2_recv, r3_send, r3_recv,
+    up_send, up_recv, down_send, down_recv, vup_send, vup_recv, vdown_send, vdown_recv,
+    q1_send, q1_recv, q2_send, q2_recv, q3_send, q3_recv,
+    v1_send, v1_recv, v2_send, v2_recv, v3_send, v3_recv,
 ):
     x = lax.axis_index("ctx")
     f = lax.axis_index("fsdp")
@@ -192,9 +194,13 @@
     rows = wq.shape[0]
     qcols = wq.shape[1] // PLANE
     kcols = wk.shape[1] // PLANE
+    acols = qcols + kcols
     piece = feats // PLANE
-    plane_rows = 4 * rows
     seq = 2 * tok
+    sub = tok // 4
+    heads = qcols // kcols
+    middle = (z > 0) & (z < chain - 1)
+    outer = (z == 0) | (z == chain - 1)
 
     def coords(r):
         px = 1 - x if r & 4 else x
@@ -213,20 +219,16 @@
     def above(pz):
         return {"ctx": x, "fsdp": (pz * 2 + y) * 2 + c}
 
-    def tok_rows(r):
-        px, py, pc = coords(r)
-        return pl.ds(pl.multiple_of(((py * 2 + pc) * 2 + px) * tok, tok), tok)
-
     def tok_slot(r):
         px, py, pc = coords(r)
         return (py * 2 + pc) * 2 + px
 
-    def tok_piece(r, part):
-        px, py, pc = coords(r)
-        if part is None:
-            return tok_rows(r)
-        begin = ((py * 2 + pc) * 2 + px) * tok + part * (tok // 2)
-        return pl.ds(pl.multiple_of(begin, tok // 2), tok // 2)
+    def tok_piece(r, low, count):
+        begin = tok_slot(r) * tok + low * sub
+        return pl.ds(pl.multiple_of(begin, sub), count * sub)
+
+    def tok_rows(r):
+        return pl.ds(pl.multiple_of(tok_slot(r) * tok, tok), tok)
 
     def remote(src, dst, send, recv, device):
         return pltpu.make_async_remote_copy(
@@ -250,9 +252,9 @@
         h = head_of(r)
         own = w_rows(0)
         return (
-            (wq.at[:, pl.ds(pl.multiple_of(h * qcols, qcols), qcols)], W.at[own, pl.ds(0, qcols)]),
-            (wk.at[:, pl.ds(pl.multiple_of(h * kcols, kcols), kcols)], W.at[own, pl.ds(qcols, kcols)]),
-            (wv.at[:, pl.ds(pl.multiple_of(h * kcols, kcols), kcols)], W.at[own, pl.ds(qcols + kcols, kcols)]),
+            (wq.at[:, pl.ds(pl.multiple_of(h * qcols, qcols), qcols)], WA.at[own, pl.ds(0, qcols)]),
+            (wk.at[:, pl.ds(pl.multiple_of(h * kcols, kcols), kcols)], WA.at[own, pl.ds(qcols, kcols)]),
+            (wv.at[:, pl.ds(pl.multiple_of(h * kcols, kcols), kcols)], WV.at[own]),
         )
 
     def g_cols(r):
@@ -265,90 +267,164 @@
     local.append(pltpu.make_async_copy(seg, SG.at[tok_slot(0)], local_sem.at[5]))
     for copy in local:
         copy.start()
+    for i in range(2):
+        local[i].wait()
     pl.semaphore_wait(barrier, PLANE - 1 + chain - 1)
+
+    def half_rows(plane, half):
+        py = y if half == 0 else 1 - y
+        return pl.ds(pl.multiple_of((plane * 4 + py * 2) * rows, 2 * rows), 2 * rows)
+
+    def quarter_rows(plane, quarter):
+        px, py, pc = coords(quarter)
+        return pl.ds(pl.multiple_of((plane * 4 + py * 2 + pc) * rows, rows), rows)
+
+    def has_up(t):
+        return (z < chain - 1) & (z - t >= 0)
+
+    def has_down(t):
+        return (z > 0) & (z + t <= chain - 1)
+
+    def from_below(t):
+        return z - 1 - t >= 0
+
+    def from_above(t):
+        return z + 1 + t <= chain - 1
+
+    def pieces_of(t):
+        return range(4) if t == 0 else range(2)
+
+    def piece_rows(plane, t, i):
+        return quarter_rows(plane, i) if t == 0 else half_rows(plane, i)
+
+    def up_copy(t, i):
+        at = WA.at[piece_rows(z - t, t, i)]
+        return remote(at, at, up_send.at[t, i], up_recv.at[t, i], above(z + 1))
+
+    def down_copy(t, i):
+        at = WA.at[piece_rows(z + t, t, i)]
+        return remote(at, at, down_send.at[t, i], down_recv.at[t, i], above(z - 1))
+
+    def up_arrival(t, i):
+        at = WA.at[piece_rows(z - 1 - t, t, i)]
+        return remote(at, at, up_send.at[t, i], up_recv.at[t, i], above(z - 1))
+
+    def down_arrival(t, i):
+        at = WA.at[piece_rows(z + 1 + t, t, i)]
+        return remote(at, at, down_send.at[t, i], down_recv.at[t, i], above(z + 1))
+
+    def vup_copy(t, half):
+        at = WV.at[half_rows(z - t, half)]
+        return remote(at, at, vup_send.at[t, half], vup_recv.at[t, half], above(z + 1))
+
+    def vdown_copy(t, half):
+        at = WV.at[half_rows(z + t, half)]
+        return remote(at, at, vdown_send.at[t, half], vdown_recv.at[t, half], above(z - 1))
+
+    def vup_arrival(t, half):
+        at = WV.at[half_rows(z - 1 - t, half)]
+        return remote(at, at, vup_send.at[t, half], vup_recv.at[t, half], above(z - 1))
+
+    def vdown_arrival(t, half):
+        at = WV.at[half_rows(z + 1 + t, half)]
+        return remote(at, at, vdown_send.at[t, half], vdown_recv.at[t, half], above(z + 1))
+
+    def send_chain(t, i):
+        @pl.when(has_up(t))
+        def _():
+            up_copy(t, i).start()
+
+        @pl.when(has_down(t))
+        def _():
+            down_copy(t, i).start()
+
+    def recv_chain(t, i):
+        @pl.when(from_below(t))
+        def _():
+            up_arrival(t, i).wait_recv()
+
+        @pl.when(from_above(t))
+        def _():
+            down_arrival(t, i).wait_recv()
+
+    def recv_half(t, half):
+        for i in (2 * half, 2 * half + 1) if t == 0 else (half,):
+            recv_chain(t, i)
+
+    def send_value_first(k):
+        @pl.when(has_up(k - 1) & jnp.logical_not(has_up(k)))
+        def _():
+            for half in range(2):
+                vup_copy(0, half).start()
+
+        @pl.when(has_down(k - 1) & jnp.logical_not(has_down(k)))
+        def _():
+            for half in range(2):
+                vdown_copy(0, half).start()
+
+    def send_value(t, half):
+        @pl.when(has_up(t))
+        def _():
+            vup_copy(t, half).start()
+
+        @pl.when(has_down(t))
+        def _():
+            vdown_copy(t, half).start()
+
+    def recv_value(t, half):
+        @pl.when(from_below(t))
+        def _():
+            vup_arrival(t, half).wait_recv()
+
+        @pl.when(from_above(t))
+        def _():
+            vdown_arrival(t, half).wait_recv()
 
     w_copies = {}
     for r in (1, 2, 3):
         w_copies[r] = [
             remote(a, b, w_send.at[r, i], w_recv.at[r, i], peer(r)) for i, (a, b) in enumerate(w_parts(r))
         ]
-        for copy in w_copies[r]:
-            copy.start()
+    for r in (1, 2, 3):
+        for i in range(2):
+            w_copies[r][i].start()
+    send_chain(0, 0)
+    w_copies[1][2].start()
+
     t_copies = []
 
-    def send_token(r_mine, r_there, hop, part=None):
-        at = N.at[tok_piece(r_mine, part)]
-        source = at
-        if r_mine == 0:
-            source = raw if part is None else raw.at[pl.ds(part * (tok // 2), tok // 2)]
-        i = part or 0
-        copy = remote(source, at, t_send.at[r_there, i], t_recv.at[r_there, i], peer(hop))
+    def send_token(r_mine, r_there, hop, low=0, count=4):
+        at = N.at[tok_piece(r_mine, low, count)]
+        source = raw.at[pl.ds(low * sub, count * sub)] if r_mine == 0 else at
+        copy = remote(source, at, t_send.at[r_there, low], t_recv.at[r_there, low], peer(hop))
         copy.start()
         t_copies.append(copy)
 
-    send_token(0, 2, 2, 0)
-    send_token(0, 2, 2, 1)
-    send_token(0, 4, 4)
+    def wait_token(r, low=0, count=4):
+        at = N.at[tok_piece(r, low, count)]
+        remote(at, at, t_send.at[r, low], t_recv.at[r, low], peer(1)).wait_recv()
+
     send_token(0, 1, 1)
+    send_token(0, 4, 4, 3, 1)
+    send_token(0, 4, 4, 0, 3)
+    for low in range(4):
+        send_token(0, 2, 2, low, 1)
     g_copies = {}
     s_copies = {}
     for r in range(1, PLANE):
         g_copies[r] = remote(g_cols(r), G.at[tok_rows(0)], g_send.at[r], g_recv.at[r], peer(r))
         s_copies[r] = remote(seg, SG.at[tok_slot(0)], s_send.at[r], s_recv.at[r], peer(r))
-
-    def half_rows(plane, half):
-        py = y if half == 0 else 1 - y
-        return pl.ds(pl.multiple_of((plane * 4 + py * 2) * rows, 2 * rows), 2 * rows)
-
-    def up_copy(t, half):
-        at = W.at[half_rows(z - t, half)]
-        return remote(at, at, up_send.at[t, half], up_recv.at[t, half], above(z + 1))
-
-    def down_copy(t, half):
-        at = W.at[half_rows(z + t, half)]
-        return remote(at, at, down_send.at[t, half], down_recv.at[t, half], above(z - 1))
-
-    def up_arrival(t, half):
-        at = W.at[half_rows(z - 1 - t, half)]
-        return remote(at, at, up_send.at[t, half], up_recv.at[t, half], above(z - 1))
-
-    def down_arrival(t, half):
-        at = W.at[half_rows(z + 1 + t, half)]
-        return remote(at, at, down_send.at[t, half], down_recv.at[t, half], above(z + 1))
-
-    def has_up(t):
-        return (z < chain - 1) & (z - t >= 0)
-
-    def has_down(t):
-        return (z > 0) & (z + t <= chain - 1)
-
-    def send_chain(t, half):
-        @pl.when(has_up(t))
-        def _():
-            up_copy(t, half).start()
-
-        @pl.when(has_down(t))
-        def _():
-            down_copy(t, half).start()
-
-    def recv_chain(t, half):
-        @pl.when(z - 1 - t >= 0)
-        def _():
-            up_arrival(t, half).wait_recv()
-
-        @pl.when(z + 1 + t <= chain - 1)
-        def _():
-            down_arrival(t, half).wait_recv()
-
-    def wait_token(r, part=None):
-        at = N.at[tok_piece(r, part)]
-        i = part or 0
-        remote(at, at, t_send.at[r, i], t_recv.at[r, i], peer(1)).wait_recv()
-
-    def wait_weight(r):
+    for r in (2, 3):
+        w_copies[r][2].start()
+
+    def wait_weight(r, value=False):
         at = w_rows(r)
-        for i, (lo, width) in enumerate(((0, qcols), (qcols, kcols), (qcols + kcols, kcols))):
-            ref = W.at[at, pl.ds(lo, width)]
+        if value:
+            ref = WV.at[at]
+            remote(ref, ref, w_send.at[r, 2], w_recv.at[r, 2], peer(r)).wait_recv()
+            return
+        for i, (lo, width) in enumerate(((0, qcols), (qcols, kcols))):
+            ref = WA.at[at, pl.ds(lo, width)]
             remote(ref, ref, w_send.at[r, i], w_recv.at[r, i], peer(r)).wait_recv()
 
     part_rows = 4 * tok
@@ -357,13 +433,16 @@
         py = y if part == 0 else 1 - y
         return pl.ds(pl.multiple_of(py * part_rows + i * height, height), height)
 
+    h = head_of(0)
+    qu_own = qu[:, pl.ds(pl.multiple_of(h * qcols, qcols), qcols)]
+    vu_own = vu[:, pl.ds(pl.multiple_of(h * kcols, kcols), kcols)]
+
     def prepare(r):
         height = tok // 2
 
         @pl.loop(0, 2)
         def _(i):
-            px, py, pc = coords(r)
-            begin = ((py * 2 + pc) * 2 + px) * tok + i * height
+            begin = tok_slot(r) * tok + i * height
             at = pl.ds(pl.multiple_of(begin, height), height)
             flt = N[at, :].astype(F32)
             meansq = jnp.sum(flt * flt, axis=-1, keepdims=True) / feats
@@ -371,88 +450,128 @@
 
         at = tok_rows(r)
         block = M[at, :]
-        LQ[at, :] = dot(block, qd[...], ((1,), (1,))).astype(BF16)
-        LV[at, :] = dot(block, vd[...], ((1,), (1,))).astype(BF16)
-
-    def add_piece(plane, half, part, first=False):
+        low_query = dot(block, qd[...], ((1,), (1,))).astype(BF16)
+        low_value = dot(block, vd[...], ((1,), (1,))).astype(BF16)
+        LQ[at, :] = low_query
+        LV[at, :] = low_value
+        acc[at, 0:qcols] = ADAPTER_NAME * dot(low_query, qu_own)
+        acc[at, qcols:] = jnp.zeros((tok, kcols), F32)
+        accv[at, :] = ADAPTER_NAME * dot(low_value, vu_own)
+
+    def add_piece(plane, half, part):
         chosen = half_rows(plane, half)
 
         @pl.loop(0, part_rows // seq)
         def _(i):
             at = part_at(part, i, seq)
-            value = dot(M[at, chosen], W[chosen, :])
-            acc[at, :] = value if first else acc[at, :] + value
+            acc[at, :] = acc[at, :] + dot(M[at, chosen], WA[chosen, :])
 
     def add_step(t, half, part):
-        @pl.when(z - 1 - t >= 0)
+        @pl.when(from_below(t))
         def _():
             add_piece(z - 1 - t, half, part)
 
-        @pl.when(z + 1 + t <= chain - 1)
+        @pl.when(from_above(t))
         def _():
             add_piece(z + 1 + t, half, part)
 
-    for i in range(3):
-        local[i].wait()
+    def add_value_piece(plane, half):
+        chosen = half_rows(plane, half)
+
+        @pl.loop(0, 2 * part_rows // seq)
+        def _(i):
+            at = pl.ds(pl.multiple_of(i * seq, seq), seq)
+            accv[at, :] = accv[at, :] + dot(M[at, chosen], WV[chosen, :])
+
+    def add_value(t, half):
+        @pl.when(from_below(t))
+        def _():
+            add_value_piece(z - 1 - t, half)
+
+        @pl.when(from_above(t))
+        def _():
+            add_value_piece(z + 1 + t, half)
+
     wait_weight(1)
-    send_chain(0, 0)
-    wait_weight(2)
-    wait_weight(3)
     send_chain(0, 1)
     for r in range(1, PLANE):
         s_copies[r].start()
-    recv_chain(0, 0)
-    send_chain(1, 0)
     local[3].wait()
     prepare(0)
     wait_token(1)
     prepare(1)
-    wait_token(4)
+    wait_weight(2)
+    send_chain(0, 2)
+    wait_weight(3)
+    send_chain(0, 3)
+    recv_half(0, 0)
+    send_chain(1, 0)
+    wait_token(2, 0, 1)
+    send_token(2, 6, 4, 0, 1)
+    recv_half(0, 1)
+    send_chain(1, 1)
+    local[2].wait()
+    wait_weight(1, True)
+    wait_weight(2, True)
+    wait_weight(3, True)
+    send_value_first(1)
+    wait_token(2, 1, 1)
+    send_token(2, 6, 4, 1, 1)
+    wait_token(4, 3, 1)
+    send_token(4, 6, 2, 3, 1)
+    wait_token(4, 0, 3)
     send_token(4, 5, 1)
-    wait_token(2, 0)
-    send_token(2, 6, 4, 0)
-    recv_chain(0, 1)
-    send_chain(1, 1)
     prepare(4)
+    wait_token(2, 2, 1)
+    send_token(2, 6, 4, 2, 1)
+    for r in (6, 7, 4, 5, 2, 3, 1):
+        g_copies[r].start()
     wait_token(5)
     prepare(5)
-    wait_token(2, 1)
-    send_token(2, 6, 4, 1)
-    send_token(2, 3, 1)
-    for r in range(1, PLANE):
-        g_copies[r].start()
-    prepare(2)
-    add_piece(z, 0, 0, True)
-    add_piece(z, 1, 0)
+    recv_half(1, 0)
+    send_chain(2, 0)
+    for half in range(2):
+        add_piece(z, half, 0)
     for half in range(2):
         add_step(0, half, 0)
+    wait_token(2, 3, 1)
+    send_token(2, 3, 1)
+    prepare(2)
     wait_token(3)
     prepare(3)
-    for t in range(1, chain - 2):
-        for half in range(2):
-            recv_chain(t, half)
-            send_chain(t + 1, half)
-            add_step(t, half, 0)
-    wait_token(6, 0)
-    wait_token(6, 1)
+    recv_half(1, 1)
+    send_chain(2, 1)
+    for k in range(2, chain):
+        send_value_first(k)
+    for half in range(2):
+        add_step(1, half, 0)
+    for low in range(4):
+        wait_token(6, low, 1)
     send_token(6, 7, 1)
     prepare(6)
     wait_token(7)
     prepare(7)
-    add_piece(z, 0, 1, True)
-    add_piece(z, 1, 1)
-    for t in range(chain - 2):
+
+    @pl.when(middle)
+    def _():
+        for half in range(2):
+            recv_value(0, half)
+            send_value(1, half)
+
+    for half in range(2):
+        add_piece(z, half, 1)
+    for t in range(2):
         for half in range(2):
             add_step(t, half, 1)
-    for half in range(2):
-        recv_chain(chain - 2, half)
-        for part in range(2):
-            add_step(chain - 2, half, part)
+    for t in range(2, chain - 1):
+        for half in range(2):
+            recv_half(t, half)
+            if t + 1 < chain - 1:
+                send_chain(t + 1, half)
+            for part in range(2):
+                add_step(t, half, part)
 
     tiles = PLANE * tok // seq
-    h = head_of(0)
-    qu_own = qu[:, pl.ds(pl.multiple_of(h * qcols, qcols), qcols)]
-    vu_own = vu[:, pl.ds(pl.multiple_of(h * kcols, kcols), kcols)]
     local[4].wait()
     local[5].wait()
     for r in range(1, PLANE):
@@ -468,9 +587,9 @@
     @pl.loop(0, tiles, unroll=2)
     def _(i):
         at = pl.ds(pl.multiple_of(i * seq, seq), seq)
-        q_all = (acc[at, 0:qcols] + ADAPTER_NAME * dot(LQ[at, :], qu_own)).astype(BF16)
-        k = acc[at, qcols:qcols + kcols].astype(BF16)
-        v = (acc[at, qcols + kcols:] + ADAPTER_NAME * dot(LV[at, :], vu_own)).astype(BF16)
+        q_all = acc[at, 0:qcols].astype(BF16)
+        k = acc[at, qcols:].astype(BF16)
+        K[at, :] = k
         g_all = G[at, :]
         traces = [SG[2 * i].astype(F32), SG[2 * i + 1].astype(F32)]
         along = jnp.concatenate(traces, axis=1)
@@ -478,65 +597,120 @@
         across = jnp.concatenate([jnp.concatenate([own, own], axis=1) for own in turned], axis=0)
         mask = band & (across == along)
         dv = jnp.zeros((seq, kcols), F32)
-        for n in range(qcols // kcols):
+        for n in range(heads):
             q = q_all[:, n * kcols:(n + 1) * kcols]
             g = g_all[:, n * kcols:(n + 1) * kcols]
             t = jnp.tanh(dot(q, k, ((1,), (1,))) * (QSCALE / CAP))
             expo = jnp.where(mask, jnp.exp(CAP * t), 0.0)
             weights = expo * (1.0 / jnp.sum(expo, axis=-1, keepdims=True))
             weights16 = weights.astype(BF16)
-            attended = dot(weights16, v)
-            dweight = dot(g, v, ((1,), (1,)))
-            delta = jnp.sum(g.astype(F32) * attended, axis=-1, keepdims=True)
-            dscore = (weights * (dweight - delta) * (1.0 - t * t)).astype(BF16)
-            DQ[at, n * kcols:(n + 1) * kcols] = (dot(dscore, k) * QSCALE).astype(BF16)
+            P[i * heads + n] = weights16
+            C[i * heads + n] = weights * (1.0 - t * t)
             dv = dv + dot(weights16, g, ((0,), (0,)))
         DV[at, :] = dv.astype(BF16)
 
-    pull_q = dot(qu_own, DQ[...], ((1,), (1,))).astype(BF16)
-    pull_v = dot(vu_own, DV[...], ((1,), (1,))).astype(BF16)
-    pull = jnp.concatenate([pull_q, pull_v], axis=0)
-    ranks = pull.shape[0]
-    half_rank = ranks // 2
-    r1_copies = []
-    for r in (7, 6, 5, 4, 3, 2, 1, 0):
-        columns = pl.ds(pl.multiple_of(head_of(r) * piece, piece), piece)
-        A[r] = dot(pull, M[:, columns]).astype(BF16)
-        if r > 0:
-            copy = remote(A.at[r], RA.at[r], r1_send.at[r], r1_recv.at[r], peer(r))
+    @pl.when(middle)
+    def _():
+        for t in range(1, chain - 1):
+            for half in range(2):
+                recv_value(t, half)
+                if t + 1 < chain - 1:
+                    send_value(t + 1, half)
+
+    def scatter(pull, part, arrived, send, recv):
+        copies = []
+        for r in (7, 6, 5, 4, 3, 2, 1, 0):
+            columns = pl.ds(pl.multiple_of(head_of(r) * piece, piece), piece)
+            part[r] = dot(pull, M[:, columns]).astype(BF16)
+            if r > 0:
+                copy = remote(part.at[r], arrived.at[r], send.at[r], recv.at[r], peer(r))
+                copy.start()
+                copies.append(copy)
+        return copies
+
+    def plane_sum(part, arrived):
+        total = part[0].astype(F32)
+        for r in range(1, PLANE):
+            total = total + arrived[r].astype(F32)
+        return total.astype(BF16)
+
+    def share(sums, send, recv):
+        own = sums.at[z]
+        copies = []
+        for d in range(1, chain):
+            copy = remote(own, own, send.at[d], recv.at[d], above((z + d) % chain))
             copy.start()
-            r1_copies.append(copy)
-    own_sum = RS.at[z]
-    own_sum[ranks:, 0:qcols] = dot(LQ[...], DQ[...], ((0,), (0,))).astype(BF16)
-    own_sum[ranks:, qcols:qcols + kcols] = dot(LV[...], DV[...], ((0,), (0,))).astype(BF16)
-    for copy in r1_copies:
+            copies.append(copy)
+        return copies
+
+    def shared(sums, send, recv):
+        for d in range(1, chain):
+            at = sums.at[(z - d + chain) % chain]
+            remote(at, at, send.at[d], recv.at[d], above((z + d) % chain)).wait_recv()
+        total = sums[0].astype(F32)
+        for d in range(1, chain):
+            total = total + sums[d].astype(F32)
+        return (total * coefficient).astype(BF16)
+
+    def spread(total, mine, out, send, recv):
+        mine[...] = total
+        copies = []
+        for r in (7, 6, 5, 4, 3, 2, 1):
+            copy = remote(mine, out.at[h], send.at[r], recv.at[r], peer(r))
+            copy.start()
+            copies.append(copy)
+        out[h] = total
+        return copies
+
+    def gathered(out, send, recv):
+        for r in range(1, PLANE):
+            at = out.at[head_of(r)]
+            remote(at, at, send.at[r], recv.at[r], peer(r)).wait_recv()
+
+    v1_copies = scatter(dot(vu_own, DV[...], ((1,), (1,))).astype(BF16), AV, RAV, v1_send, v1_recv)
+    RSV.at[z][:, piece:] = dot(LV[...], DV[...], ((0,), (0,))).astype(BF16)
+    for half in range(2):
+        add_value_piece(z, half)
+    for t in range(chain - 2):
+        for half in range(2):
+            @pl.when(outer)
+            def _():
+                recv_value(t, half)
+
+            add_value(t, half)
+    for copy in v1_copies:
         copy.wait_recv()
-    total = A[0].astype(F32)
-    for r in range(1, PLANE):
-        total = total + RA[r].astype(F32)
-    own_sum[0:ranks, :] = total.astype(BF16)
-    r2_copies = []
-    for d in range(1, chain):
-        copy = remote(own_sum, own_sum, r2_send.at[d], r2_recv.at[d], above((z + d) % chain))
-        copy.start()
-        r2_copies.append(copy)
-    for d in range(1, chain):
-        at = RS.at[(z - d + chain) % chain]
-        remote(at, at, r2_send.at[d], r2_recv.at[d], above((z + d) % chain)).wait_recv()
-    total = RS[0].astype(F32)
-    for d in range(1, chain):
-        total = total + RS[d].astype(F32)
-    total = (total * coefficient).astype(BF16)
-    T[...] = total
-    r3_copies = []
-    for r in (7, 6, 5, 4, 3, 2, 1):
-        copy = remote(T, OUT.at[h], r3_send.at[r], r3_recv.at[r], peer(r))
-        copy.start()
-        r3_copies.append(copy)
-    OUT[h] = total
-    for r in range(1, PLANE):
-        at = OUT.at[head_of(r)]
-        remote(at, at, r3_send.at[r], r3_recv.at[r], peer(r)).wait_recv()
+    RSV.at[z][:, 0:piece] = plane_sum(AV, RAV)
+    v2_copies = share(RSV, v2_send, v2_recv)
+    for half in range(2):
+        @pl.when(outer)
+        def _():
+            recv_value(chain - 2, half)
+
+        add_value(chain - 2, half)
+
+    @pl.loop(0, tiles, unroll=2)
+    def _(i):
+        at = pl.ds(pl.multiple_of(i * seq, seq), seq)
+        v = accv[at, :].astype(BF16)
+        k = K[at, :]
+        for n in range(heads):
+            g = G[at, n * kcols:(n + 1) * kcols]
+            dweight = dot(g, v, ((1,), (1,)))
+            delta = jnp.sum(P[i * heads + n].astype(F32) * dweight, axis=-1, keepdims=True)
+            dscore = (C[i * heads + n] * (dweight - delta)).astype(BF16)
+            DQ[at, n * kcols:(n + 1) * kcols] = (dot(dscore, k) * QSCALE).astype(BF16)
+
+    q1_copies = scatter(dot(qu_own, DQ[...], ((1,), (1,))).astype(BF16), AQ, RAQ, q1_send, q1_recv)
+    RSQ.at[z][:, piece:] = dot(LQ[...], DQ[...], ((0,), (0,))).astype(BF16)
+    v3_copies = spread(shared(RSV, v2_send, v2_recv), TV, OUTV, v3_send, v3_recv)
+    for copy in q1_copies:
+        copy.wait_recv()
+    RSQ.at[z][:, 0:piece] = plane_sum(AQ, RAQ)
+    q2_copies = share(RSQ, q2_send, q2_recv)
+    q3_copies = spread(shared(RSQ, q2_send, q2_recv), TQ, OUTQ, q3_send, q3_recv)
+    gathered(OUTV, v3_send, v3_recv)
+    gathered(OUTQ, q3_send, q3_recv)
 
     for r in (1, 2, 3):
         for copy in w_copies[r]:
@@ -547,29 +721,35 @@
         g_copies[r].wait_send()
         s_copies[r].wait_send()
     for t in range(chain - 1):
-        for half in range(2):
-            @pl.when(has_up(t))
-            def _():
-                up_copy(t, half).wait_send()
-
-            @pl.when(has_down(t))
-            def _():
-                down_copy(t, half).wait_send()
-    for copy in r1_copies + r2_copies + r3_copies:
+        @pl.when(has_up(t))
+        def _():
+            for i in pieces_of(t):
+                up_copy(t, i).wait_send()
+            for half in range(2):
+                vup_copy(t, half).wait_send()
+
+        @pl.when(has_down(t))
+        def _():
+            for i in pieces_of(t):
+                down_copy(t, i).wait_send()
+            for half in range(2):
+                vdown_copy(t, half).wait_send()
+    for copy in v1_copies + v2_copies + v3_copies + q1_copies + q2_copies + q3_copies:
         copy.wait_send()
 
 
-def unpack_kernel(gathered, out_aq, out_bq, out_av, out_bv):
-    ranks, feats = out_aq.shape
+def unpack_kernel(outq, outv, out_aq, out_bq, out_av, out_bv):
+    feats = out_aq.shape[1]
     piece = feats // PLANE
     qcols = out_bq.shape[1] // PLANE
     kcols = out_bv.shape[1] // PLANE
     for h in range(PLANE):
-        value = gathered[h].astype(F32)
-        out_aq[:, h * piece:(h + 1) * piece] = value[0:ranks]
-        out_av[:, h * piece:(h + 1) * piece] = value[ranks:2 * ranks]
-        out_bq[:, h * qcols:(h + 1) * qcols] = value[2 * ranks:, 0:qcols]
-        out_bv[:, h * kcols:(h + 1) * kcols] = value[2 * ranks:, qcols:qcols + kcols]
+        value = outq[h].astype(F32)
+        out_aq[:, h * piece:(h + 1) * piece] = value[:, 0:piece]
+        out_bq[:, h * qcols:(h + 1) * qcols] = value[:, piece:]
+        value = outv[h].astype(F32)
+        out_av[:, h * piece:(h + 1) * piece] = value[:, 0:piece]
+        out_bv[:, h * kcols:(h + 1) * kcols] = value[:, piece:]
 
 
 def on_plane(
@@ -592,40 +772,55 @@
     ranks = query_down_weight.shape[1]
     qcols = query_weight.shape[1] // PLANE
     kcols = key_weight.shape[1] // PLANE
-    columns = qcols + 2 * kcols
     piece = feats // PLANE
     many = PLANE * tok
     token_total = lax.axis_size("ctx") * fsdp * tok
     coefficient = ADAPTER_NAME / math.sqrt(token_total)
-    hbm = pl.BlockSpec(memory_space=pl.ANY)
+    hbm = pl.BlockSpec(memory_space=pltpu.HBM)
     vmem = pl.BlockSpec(memory_space=pltpu.VMEM)
     dma = pltpu.SemaphoreType.DMA
-    steps = max(chain - 1, 1)
-    gathered = pl.pallas_call(
+    steps = chain - 1
+    tiles = many // (2 * tok)
+    heads = qcols // kcols
+    outq, outv = pl.pallas_call(
         functools.partial(plane_kernel, chain, coefficient),
-        out_shape=jax.ShapeDtypeStruct((PLANE, 3 * ranks, piece), BF16),
+        out_shape=(
+            jax.ShapeDtypeStruct((PLANE, ranks, piece + qcols), BF16),
+            jax.ShapeDtypeStruct((PLANE, ranks, piece + kcols), BF16),
+        ),
         in_specs=[hbm, hbm, vmem, hbm, hbm, hbm, vmem, vmem, vmem, vmem, hbm],
-        out_specs=vmem,
+        out_specs=(vmem, vmem),
         scratch_shapes=[
             pltpu.VMEM((many, feats), BF16),
             pltpu.VMEM((many, feats), BF16),
-            pltpu.VMEM((feats, columns), BF16),
+            pltpu.VMEM((feats, qcols + kcols), BF16),
+            pltpu.VMEM((feats, kcols), BF16),
             pltpu.VMEM((many, qcols), BF16),
             pltpu.VMEM((PLANE, 1, tok), jnp.int32),
-            pltpu.VMEM((many, columns), F32),
+            pltpu.VMEM((many, qcols + kcols), F32),
+            pltpu.VMEM((many, kcols), F32),
+            pltpu.VMEM((tiles * heads, 2 * tok, 2 * tok), BF16),
+            pltpu.VMEM((tiles * heads, 2 * tok, 2 * tok), F32),
+            pltpu.VMEM((many, kcols), BF16),
             pltpu.VMEM((many, qcols), BF16),
             pltpu.VMEM((many, kcols), BF16),
             pltpu.VMEM((many, ranks), BF16),
             pltpu.VMEM((many, ranks), BF16),
-            pltpu.VMEM((PLANE, 2 * ranks, piece), BF16),
-            pltpu.VMEM((PLANE, 2 * ranks, piece), BF16),
-            pltpu.VMEM((chain, 3 * ranks, piece), BF16),
-            pltpu.VMEM((3 * ranks, piece), BF16),
+            pltpu.VMEM((PLANE, ranks, piece), BF16),
+            pltpu.VMEM((PLANE, ranks, piece), BF16),
+            pltpu.VMEM((chain, ranks, piece + qcols), BF16),
+            pltpu.VMEM((ranks, piece + qcols), BF16),
+            pltpu.VMEM((PLANE, ranks, piece), BF16),
+            pltpu.VMEM((PLANE, ranks, piece), BF16),
+            pltpu.VMEM((chain, ranks, piece + kcols), BF16),
+            pltpu.VMEM((ranks, piece + kcols), BF16),
             dma((6,)),
             dma((4, 3)), dma((4, 3)),
-            dma((8, 2)), dma((8, 2)), dma((8,)), dma((8,)), dma((8,)), dma((8,)),
+            dma((8, 4)), dma((8, 4)), dma((8,)), dma((8,)), dma((8,)), dma((8,)),
+            dma((steps, 4)), dma((steps, 4)), dma((steps, 4)), dma((steps, 4)),
             dma((steps, 2)), dma((steps, 2)), dma((steps, 2)), dma((steps, 2)),
-            dma((8,)), dma((8,)), dma((max(chain, 2),)), dma((max(chain, 2),)), dma((8,)), dma((8,)),
+            dma((8,)), dma((8,)), dma((chain,)), dma((chain,)), dma((8,)), dma((8,)),
+            dma((8,)), dma((8,)), dma((chain,)), dma((chain,)), dma((8,)), dma((8,)),
         ],
         compiler_params=pltpu.CompilerParams(
             collective_id=0, has_side_effects=True, vmem_limit_bytes=56 * 1024 * 1024
@@ -644,9 +839,10 @@
             jax.ShapeDtypeStruct((ranks, feats), F32),
             jax.ShapeDtypeStruct((ranks, value_weight.shape[1]), F32),
         ),
-        in_specs=[vmem],
+        in_specs=[vmem, vmem],
         out_specs=(vmem, vmem, vmem, vmem),
-    )(gathered)
+        compiler_params=pltpu.CompilerParams(vmem_limit_bytes=16 * 1024 * 1024),
+    )(outq, outv)
     return (aq.T, bq, av.T, bv)
 
 

time: 84.4 us -> 84.5 us (level)
  local copies, waits for them, and re-layouts: 0 us -> 1.81 us
  Pallas kernels: 83.6 us -> 81.8 us
    unnamed x0 -> x4, local copies, waits for them, and re-layouts: none -> 1.81 us
    pallas_call x1, Pallas kernels: 1.78 us -> 0.81 us  [on_plane(): pl.pallas_call(unpack_kernel, out_shape=(jax.ShapeDtypeStruct((ranks, fea...]
where the time goes in v1:
time: 84.5 us; the launch traced here: 84.3 us
  Pallas kernels  81.8 us (97%)
  local copies, waits for them, and re-layouts  1.81 us (2%)
    pallas_call x1, Pallas kernels, on_plane(): pl.pallas_call(functools.partial(plane_kernel, chain, coefficient), out_s...  81 us
    unnamed x4, local copies, waits for them, and re-layouts  1.81 us

profile of v1, /device:TPU:0, one launch (start us, length us, event | category | flops | bytes accessed | tf_op | source)
XLA Modules:
  0.0 84.3 jit_solution(9396772561934330894)
XLA Ops:
  0.6 81.0 %shard_map.138 = (bf16[8,16,640]{2,1,0:T(8,128)(2,1)}, bf16[8,16,512]{2,1,0:T(8,128)(2,1)}) custom-call(bf16[128,3072]{1,0:T(8,128)(2,1)} %bitcast.6, s32[1,128]{1,0:T(1,128)} %seg.1, bf16[3072]{0:T(1024)(128)(2,1)} %gain.1, bf16[192,2048]{1,0:T(8,128)(2,1)} %wq.1, bf16[192,1024]{1,0:T(8,128)(2,1)} %wk.1, bf16[192,1024]{1,0:T(8,128)(2,1)} %wv.1, ...), custom_call_target="tpu_custom_call" | custom-call | tf_op jit(solution)/shard_map/pallas_call | solution.py:785
  81.6 0.0 copy-start
  81.7 0.9 %copy-done = bf16[8,16,640]{2,1,0:T(8,128)(2,1)S(1)} copy-done((bf16[8,16,640]{2,1,0:T(8,128)(2,1)S(1)}, bf16[8,16,640]{2,1,0:T(8,128)(2,1)}, u32[]{:S(2)}) %copy-start) | copy-done | bytes 163864
  82.6 0.0 copy-start.1
  82.6 0.9 %copy-done.1 = bf16[8,16,512]{2,1,0:T(8,128)(2,1)S(1)} copy-done((bf16[8,16,512]{2,1,0:T(8,128)(2,1)S(1)}, bf16[8,16,512]{2,1,0:T(8,128)(2,1)}, u32[]{:S(2)}) %copy-start.1) | copy-done | bytes 131096
  83.5 0.8 shard_map.139
Async XLA Ops:
  81.6 0.9 %copy-start = (bf16[8,16,640]{2,1,0:T(8,128)(2,1)S(1)}, bf16[8,16,640]{2,1,0:T(8,128)(2,1)}, u32[]{:S(2)}) copy-start(bf16[8,16,640]{2,1,0:T(8,128)(2,1)} %get-tuple-element.10.outq) | copy-start | bytes 491524
  82.6 0.9 %copy-start.1 = (bf16[8,16,512]{2,1,0:T(8,128)(2,1)S(1)}, bf16[8,16,512]{2,1,0:T(8,128)(2,1)}, u32[]{:S(2)}) copy-start(bf16[8,16,512]{2,1,0:T(8,128)(2,1)} %get-tuple-element.11.outv) | copy-start | bytes 393220

commit v2 on v1

--- a/solution.py
+++ b/solution.py
@@ -389,7 +389,8 @@
         for i in range(2):
             w_copies[r][i].start()
     send_chain(0, 0)
-    w_copies[1][2].start()
+    for r in (1, 2, 3):
+        w_copies[r][2].start()
 
     t_copies = []
 
@@ -414,8 +415,6 @@
     for r in range(1, PLANE):
         g_copies[r] = remote(g_cols(r), G.at[tok_rows(0)], g_send.at[r], g_recv.at[r], peer(r))
         s_copies[r] = remote(seg, SG.at[tok_slot(0)], s_send.at[r], s_recv.at[r], peer(r))
-    for r in (2, 3):
-        w_copies[r][2].start()
 
     def wait_weight(r, value=False):
         at = w_rows(r)
@@ -785,8 +784,8 @@
     outq, outv = pl.pallas_call(
         functools.partial(plane_kernel, chain, coefficient),
         out_shape=(
-            jax.ShapeDtypeStruct((PLANE, ranks, piece + qcols), BF16),
-            jax.ShapeDtypeStruct((PLANE, ranks, piece + kcols), BF16),
+            pltpu.VMEM((PLANE, ranks, piece + qcols), BF16),
+            pltpu.VMEM((PLANE, ranks, piece + kcols), BF16),
         ),
         in_specs=[hbm, hbm, vmem, hbm, hbm, hbm, vmem, vmem, vmem, vmem, hbm],
         out_specs=(vmem, vmem),

time: 84.5 us -> 77.9 us (0.922)
  Pallas kernels: 81.8 us -> 77.1 us
  local copies, waits for them, and re-layouts: 1.81 us -> 0 us
    pallas_call x1, Pallas kernels: 81 us -> 76.3 us  [on_plane(): pl.pallas_call(functools.partial(plane_kernel, chain, coefficient), out_s...]
    unnamed x4 -> x0, local copies, waits for them, and re-layouts: 1.81 us -> none
where the time goes in v2:
time: 77.9 us; the launch traced here: 77.8 us
  Pallas kernels  77.1 us (99%)
    pallas_call x1, Pallas kernels, on_plane(): pl.pallas_call(functools.partial(plane_kernel, chain, coefficient), out_s...  76.3 us

profile of v2, /device:TPU:0, one launch (start us, length us, event | category | flops | bytes accessed | tf_op | source)
XLA Modules:
  0.0 77.8 jit_solution(4673317922852042663)
XLA Ops:
  0.6 76.3 %shard_map.138 = (bf16[8,16,640]{2,1,0:T(8,128)(2,1)S(1)}, bf16[8,16,512]{2,1,0:T(8,128)(2,1)S(1)}) custom-call(bf16[128,3072]{1,0:T(8,128)(2,1)} %bitcast.6, s32[1,128]{1,0:T(1,128)} %seg.1, bf16[3072]{0:T(1024)(128)(2,1)} %gain.1, bf16[192,2048]{1,0:T(8,128)(2,1)} %wq.1, bf16[192,1024]{1,0:T(8,128)(2,1)} %wk.1, bf16[192,1024]{1,0:T(8,128)(2,1)} %wv.1, ...), custom_call_target="tpu_custom_call" | custom-call | tf_op jit(solution)/shard_map/pallas_call | solution.py:784
  77.0 0.8 %shard_map.139 = (f32[16,3072]{1,0:T(8,128)}, f32[16,2048]{1,0:T(8,128)}, f32[16,3072]{1,0:T(8,128)}, f32[16,1024]{1,0:T(8,128)}) custom-call(bf16[8,16,640]{2,1,0:T(8,128)(2,1)S(1)} %get-tuple-element.10.outq, bf16[8,16,512]{2,1,0:T(8,128)(2,1)S(1)} %get-tuple-element.11.outv), custom_call_target="tpu_custom_call" | custom-call | tf_op jit(solution)/shard_map/pallas_call | solution.py:833

commit v3 on v2

--- a/solution.py
+++ b/solution.py
@@ -176,14 +176,14 @@
 
 def plane_kernel(
     chain, coefficient,
-    raw, seg, gain, wq, wk, wv, qd, qu, vd, vu, grad,
-    OUTQ, OUTV,
-    N, M, WA, WV, G, SG, acc, accv, P, C, K, DQ, DV, LQ, LV,
-    AQ, RAQ, RSQ, TQ, AV, RAV, RSV, TV,
-    local_sem, w_send, w_recv, t_send, t_recv, g_send, g_recv, s_send, s_recv,
+    raw, seg, gain_in, wq, wk, wv, qd, qu_in, vd, vu_in, grad,
+    OUTA, OUTB, OUTV,
+    N, M, WA, WV, G, SG, acc, accv, P, C, K, DQ, DV, LL,
+    gain, down, qu, vu,
+    PQ, RPQ, PV, RPV, RSA, RSB, RSV, TA, TB, TV,
+    local_sem, w_send, w_recv, t_send, t_recv, g_sem, s_sem,
     up_send, up_recv, down_send, down_recv, vup_send, vup_recv, vdown_send, vdown_recv,
-    q1_send, q1_recv, q2_send, q2_recv, q3_send, q3_recv,
-    v1_send, v1_recv, v2_send, v2_recv, v3_send, v3_recv,
+    q1_send, q1_recv, v1_send, v1_recv, a_sem, b_sem, v_sem,
 ):
     x = lax.axis_index("ctx")
     f = lax.axis_index("fsdp")
@@ -199,6 +199,7 @@
     seq = 2 * tok
     sub = tok // 4
     heads = qcols // kcols
+    ranks = qd.shape[0]
     middle = (z > 0) & (z < chain - 1)
     outer = (z == 0) | (z == chain - 1)
 
@@ -265,6 +266,11 @@
     local.append(pltpu.make_async_copy(raw, N.at[tok_rows(0)], local_sem.at[3]))
     local.append(pltpu.make_async_copy(g_cols(0), G.at[tok_rows(0)], local_sem.at[4]))
     local.append(pltpu.make_async_copy(seg, SG.at[tok_slot(0)], local_sem.at[5]))
+    local.append(pltpu.make_async_copy(qd, down.at[pl.ds(0, ranks)], local_sem.at[6]))
+    local.append(pltpu.make_async_copy(vd, down.at[pl.ds(ranks, ranks)], local_sem.at[7]))
+    local.append(pltpu.make_async_copy(qu_in, qu, local_sem.at[8]))
+    local.append(pltpu.make_async_copy(vu_in, vu, local_sem.at[9]))
+    local.append(pltpu.make_async_copy(gain_in, gain, local_sem.at[10]))
     for copy in local:
         copy.start()
     for i in range(2):
@@ -297,37 +303,43 @@
     def piece_rows(plane, t, i):
         return quarter_rows(plane, i) if t == 0 else half_rows(plane, i)
 
+    def half_of(t, i):
+        return i // 2 if t == 0 else i
+
+    def plane_rows(plane):
+        return pl.ds(pl.multiple_of(plane * 4 * rows, 4 * rows), 4 * rows)
+
     def up_copy(t, i):
         at = WA.at[piece_rows(z - t, t, i)]
-        return remote(at, at, up_send.at[t, i], up_recv.at[t, i], above(z + 1))
+        return remote(at, at, up_send.at[t], up_recv.at[t, half_of(t, i)], above(z + 1))
 
     def down_copy(t, i):
         at = WA.at[piece_rows(z + t, t, i)]
-        return remote(at, at, down_send.at[t, i], down_recv.at[t, i], above(z - 1))
-
-    def up_arrival(t, i):
-        at = WA.at[piece_rows(z - 1 - t, t, i)]
-        return remote(at, at, up_send.at[t, i], up_recv.at[t, i], above(z - 1))
-
-    def down_arrival(t, i):
-        at = WA.at[piece_rows(z + 1 + t, t, i)]
-        return remote(at, at, down_send.at[t, i], down_recv.at[t, i], above(z + 1))
+        return remote(at, at, down_send.at[t], down_recv.at[t, half_of(t, i)], above(z - 1))
+
+    def up_arrival(t, half):
+        at = WA.at[half_rows(z - 1 - t, half)]
+        return remote(at, at, up_send.at[t], up_recv.at[t, half], above(z - 1))
+
+    def down_arrival(t, half):
+        at = WA.at[half_rows(z + 1 + t, half)]
+        return remote(at, at, down_send.at[t], down_recv.at[t, half], above(z + 1))
 
     def vup_copy(t, half):
         at = WV.at[half_rows(z - t, half)]
-        return remote(at, at, vup_send.at[t, half], vup_recv.at[t, half], above(z + 1))
+        return remote(at, at, vup_send.at[t], vup_recv.at[t, half], above(z + 1))
 
     def vdown_copy(t, half):
         at = WV.at[half_rows(z + t, half)]
-        return remote(at, at, vdown_send.at[t, half], vdown_recv.at[t, half], above(z - 1))
+        return remote(at, at, vdown_send.at[t], vdown_recv.at[t, half], above(z - 1))
 
     def vup_arrival(t, half):
         at = WV.at[half_rows(z - 1 - t, half)]
-        return remote(at, at, vup_send.at[t, half], vup_recv.at[t, half], above(z - 1))
+        return remote(at, at, vup_send.at[t], vup_recv.at[t, half], above(z - 1))
 
     def vdown_arrival(t, half):
         at = WV.at[half_rows(z + 1 + t, half)]
-        return remote(at, at, vdown_send.at[t, half], vdown_recv.at[t, half], above(z + 1))
+        return remote(at, at, vdown_send.at[t], vdown_recv.at[t, half], above(z + 1))
 
     def send_chain(t, i):
         @pl.when(has_up(t))
@@ -338,18 +350,14 @@
         def _():
             down_copy(t, i).start()
 
-    def recv_chain(t, i):
+    def recv_half(t, half):
         @pl.when(from_below(t))
         def _():
-            up_arrival(t, i).wait_recv()
+            up_arrival(t, half).wait_recv()
 
         @pl.when(from_above(t))
         def _():
-            down_arrival(t, i).wait_recv()
-
-    def recv_half(t, half):
-        for i in (2 * half, 2 * half + 1) if t == 0 else (half,):
-            recv_chain(t, i)
+            down_arrival(t, half).wait_recv()
 
     def send_value_first(k):
         @pl.when(has_up(k - 1) & jnp.logical_not(has_up(k)))
@@ -383,7 +391,8 @@
     w_copies = {}
     for r in (1, 2, 3):
         w_copies[r] = [
-            remote(a, b, w_send.at[r, i], w_recv.at[r, i], peer(r)) for i, (a, b) in enumerate(w_parts(r))
+            remote(a, b, w_send.at[i // 2], w_recv.at[r if i < 2 else 0], peer(r))
+            for i, (a, b) in enumerate(w_parts(r))
         ]
     for r in (1, 2, 3):
         for i in range(2):
@@ -392,18 +401,19 @@
     for r in (1, 2, 3):
         w_copies[r][2].start()
 
-    t_copies = []
+    t_slot = {(1, 0): 0, (4, 3): 1, (4, 0): 2, (5, 0): 3, (3, 0): 4, (7, 0): 5}
+    for low in range(4):
+        t_slot[2, low] = 6 + low
+        t_slot[6, low] = 10
 
     def send_token(r_mine, r_there, hop, low=0, count=4):
         at = N.at[tok_piece(r_mine, low, count)]
         source = raw.at[pl.ds(low * sub, count * sub)] if r_mine == 0 else at
-        copy = remote(source, at, t_send.at[r_there, low], t_recv.at[r_there, low], peer(hop))
-        copy.start()
-        t_copies.append(copy)
+        remote(source, at, t_send.at[0], t_recv.at[t_slot[r_there, low]], peer(hop)).start()
 
     def wait_token(r, low=0, count=4):
         at = N.at[tok_piece(r, low, count)]
-        remote(at, at, t_send.at[r, low], t_recv.at[r, low], peer(1)).wait_recv()
+        remote(at, at, t_send.at[0], t_recv.at[t_slot[r, low]], peer(1)).wait_recv()
 
     send_token(0, 1, 1)
     send_token(0, 4, 4, 3, 1)
@@ -413,18 +423,16 @@
     g_copies = {}
     s_copies = {}
     for r in range(1, PLANE):
-        g_copies[r] = remote(g_cols(r), G.at[tok_rows(0)], g_send.at[r], g_recv.at[r], peer(r))
-        s_copies[r] = remote(seg, SG.at[tok_slot(0)], s_send.at[r], s_recv.at[r], peer(r))
-
-    def wait_weight(r, value=False):
-        at = w_rows(r)
-        if value:
-            ref = WV.at[at]
-            remote(ref, ref, w_send.at[r, 2], w_recv.at[r, 2], peer(r)).wait_recv()
-            return
-        for i, (lo, width) in enumerate(((0, qcols), (qcols, kcols))):
-            ref = WA.at[at, pl.ds(lo, width)]
-            remote(ref, ref, w_send.at[r, i], w_recv.at[r, i], peer(r)).wait_recv()
+        g_copies[r] = remote(g_cols(r), G.at[tok_rows(0)], g_sem.at[0], g_sem.at[1], peer(r))
+        s_copies[r] = remote(seg, SG.at[tok_slot(0)], s_sem.at[0], s_sem.at[1], peer(r))
+
+    def wait_weight(r):
+        ref = WA.at[w_rows(r)]
+        remote(ref, ref, w_send.at[0], w_recv.at[r], peer(r)).wait_recv()
+
+    def wait_values():
+        ref = WV.at[pl.ds(0, 3 * rows)]
+        remote(ref, ref, w_send.at[1], w_recv.at[0], peer(1)).wait_recv()
 
     part_rows = 4 * tok
 
@@ -433,8 +441,12 @@
         return pl.ds(pl.multiple_of(py * part_rows + i * height, height), height)
 
     h = head_of(0)
-    qu_own = qu[:, pl.ds(pl.multiple_of(h * qcols, qcols), qcols)]
-    vu_own = vu[:, pl.ds(pl.multiple_of(h * kcols, kcols), kcols)]
+
+    def query_up():
+        return qu[:, pl.ds(pl.multiple_of(h * qcols, qcols), qcols)]
+
+    def value_up():
+        return vu[:, pl.ds(pl.multiple_of(h * kcols, kcols), kcols)]
 
     def prepare(r):
         height = tok // 2
@@ -449,13 +461,12 @@
 
         at = tok_rows(r)
         block = M[at, :]
-        low_query = dot(block, qd[...], ((1,), (1,))).astype(BF16)
-        low_value = dot(block, vd[...], ((1,), (1,))).astype(BF16)
-        LQ[at, :] = low_query
-        LV[at, :] = low_value
-        acc[at, 0:qcols] = ADAPTER_NAME * dot(low_query, qu_own)
+        low = dot(block, down[...], ((1,), (1,))).astype(BF16)
+        LL[at, :] = low
+        filler = jnp.zeros((ranks, qcols), BF16)
+        acc[at, 0:qcols] = ADAPTER_NAME * dot(low, jnp.concatenate([query_up(), filler], axis=0))
         acc[at, qcols:] = jnp.zeros((tok, kcols), F32)
-        accv[at, :] = ADAPTER_NAME * dot(low_value, vu_own)
+        accv[at, :] = ADAPTER_NAME * dot(low, jnp.concatenate([filler[:, 0:kcols], value_up()], axis=0))
 
     def add_piece(plane, half, part):
         chosen = half_rows(plane, half)
@@ -496,6 +507,8 @@
     for r in range(1, PLANE):
         s_copies[r].start()
     local[3].wait()
+    for i in range(6, 11):
+        local[i].wait()
     prepare(0)
     wait_token(1)
     prepare(1)
@@ -510,9 +523,7 @@
     recv_half(0, 1)
     send_chain(1, 1)
     local[2].wait()
-    wait_weight(1, True)
-    wait_weight(2, True)
-    wait_weight(3, True)
+    wait_values()
     send_value_first(1)
     wait_token(2, 1, 1)
     send_token(2, 6, 4, 1, 1)
@@ -544,8 +555,7 @@
         send_value_first(k)
     for half in range(2):
         add_step(1, half, 0)
-    for low in range(4):
-        wait_token(6, low, 1)
+    wait_token(6)
     send_token(6, 7, 1)
     prepare(6)
     wait_token(7)
@@ -573,11 +583,12 @@
     tiles = PLANE * tok // seq
     local[4].wait()
     local[5].wait()
-    for r in range(1, PLANE):
-        at = G.at[tok_rows(r)]
-        remote(at, at, g_send.at[r], g_recv.at[r], peer(r)).wait_recv()
-        at = SG.at[tok_slot(r)]
-        remote(at, at, s_send.at[r], s_recv.at[r], peer(r)).wait_recv()
+    g_others = G.at[pl.ds(0, (PLANE - 1) * tok)]
+    g_all_copies = remote(g_others, g_others, g_sem.at[0], g_sem.at[1], peer(1))
+    g_all_copies.wait_recv()
+    s_others = SG.at[pl.ds(0, PLANE - 1)]
+    s_all_copies = remote(s_others, s_others, s_sem.at[0], s_sem.at[1], peer(1))
+    s_all_copies.wait_recv()
 
     pos_i = lax.broadcasted_iota(jnp.int32, (seq, seq), 0)
     pos_j = lax.broadcasted_iota(jnp.int32, (seq, seq), 1)
@@ -616,58 +627,62 @@
                 if t + 1 < chain - 1:
                     send_value(t + 1, half)
 
-    def scatter(pull, part, arrived, send, recv):
-        copies = []
-        for r in (7, 6, 5, 4, 3, 2, 1, 0):
-            columns = pl.ds(pl.multiple_of(head_of(r) * piece, piece), piece)
-            part[r] = dot(pull, M[:, columns]).astype(BF16)
-            if r > 0:
-                copy = remote(part.at[r], arrived.at[r], send.at[r], recv.at[r], peer(r))
-                copy.start()
-                copies.append(copy)
-        return copies
-
-    def plane_sum(part, arrived):
-        total = part[0].astype(F32)
-        for r in range(1, PLANE):
-            total = total + arrived[r].astype(F32)
+    half_tokens = PLANE * tok // 2
+
+    def token_half(half):
+        return pl.ds(half * half_tokens, half_tokens)
+
+    def send_pull(half, up, change, mine, arrived, send, recv):
+        mine[half] = dot(up, change[token_half(half), :], ((1,), (1,))).astype(BF16)
+        for r in (7, 6, 5, 4, 3, 2, 1):
+            remote(mine.at[half], arrived.at[half, r], send.at[half], recv.at[half], peer(r)).start()
+
+    def pulls(half, arrived, send, recv):
+        at = arrived.at[half, pl.ds(1, PLANE - 1)]
+        return remote(at, at, send.at[half], recv.at[half], peer(1))
+
+    own_columns = pl.ds(pl.multiple_of(h * piece, piece), piece)
+
+    def down_gradient(mine, arrived, send, recv):
+        total = jnp.zeros((ranks, piece), F32)
+        for half in range(2):
+            pulls(half, arrived, send, recv).wait_recv()
+            pull = mine[half].astype(F32)
+            for r in range(1, PLANE):
+                pull = pull + arrived[half, r].astype(F32)
+            total = total + dot(pull.astype(BF16), M[token_half(half), own_columns])
         return total.astype(BF16)
 
-    def share(sums, send, recv):
+    def share(sums, sem):
         own = sums.at[z]
-        copies = []
         for d in range(1, chain):
-            copy = remote(own, own, send.at[d], recv.at[d], above((z + d) % chain))
-            copy.start()
-            copies.append(copy)
-        return copies
-
-    def shared(sums, send, recv):
-        for d in range(1, chain):
-            at = sums.at[(z - d + chain) % chain]
-            remote(at, at, send.at[d], recv.at[d], above((z + d) % chain)).wait_recv()
+            remote(own, own, sem.at[0], sem.at[1], above((z + d) % chain)).start()
+
+    def shares(sums, sem):
+        at = sums.at[pl.ds(0, chain - 1)]
+        return remote(at, at, sem.at[0], sem.at[1], peer(1))
+
+    def shared(sums, sem):
+        shares(sums, sem).wait_recv()
         total = sums[0].astype(F32)
         for d in range(1, chain):
             total = total + sums[d].astype(F32)
         return (total * coefficient).astype(BF16)
 
-    def spread(total, mine, out, send, recv):
+    def spread(total, mine, out, sem):
         mine[...] = total
-        copies = []
         for r in (7, 6, 5, 4, 3, 2, 1):
-            copy = remote(mine, out.at[h], send.at[r], recv.at[r], peer(r))
-            copy.start()
-            copies.append(copy)
+            remote(mine, out.at[h], sem.at[2], sem.at[3], peer(r)).start()
         out[h] = total
-        return copies
-
-    def gathered(out, send, recv):
-        for r in range(1, PLANE):
-            at = out.at[head_of(r)]
-            remote(at, at, send.at[r], recv.at[r], peer(r)).wait_recv()
-
-    v1_copies = scatter(dot(vu_own, DV[...], ((1,), (1,))).astype(BF16), AV, RAV, v1_send, v1_recv)
-    RSV.at[z][:, piece:] = dot(LV[...], DV[...], ((0,), (0,))).astype(BF16)
+
+    def spreads(out, sem):
+        at = out.at[pl.ds(0, PLANE - 1)]
+        return remote(at, at, sem.at[2], sem.at[3], peer(1))
+
+    for half in range(2):
+        send_pull(half, value_up(), DV, PV, RPV, v1_send, v1_recv)
+    low_gradient = dot(LL[...], DV[...], ((0,), (0,)))
+    RSV.at[z][:, piece:] = low_gradient[ranks:, :].astype(BF16)
     for half in range(2):
         add_value_piece(z, half)
     for t in range(chain - 2):
@@ -677,10 +692,8 @@
                 recv_value(t, half)
 
             add_value(t, half)
-    for copy in v1_copies:
-        copy.wait_recv()
-    RSV.at[z][:, 0:piece] = plane_sum(AV, RAV)
-    v2_copies = share(RSV, v2_send, v2_recv)
+    RSV.at[z][:, 0:piece] = down_gradient(PV, RPV, v1_send, v1_recv)
+    share(RSV, v_sem)
     for half in range(2):
         @pl.when(outer)
         def _():
@@ -688,64 +701,70 @@
 
         add_value(chain - 2, half)
 
-    @pl.loop(0, tiles, unroll=2)
-    def _(i):
-        at = pl.ds(pl.multiple_of(i * seq, seq), seq)
-        v = accv[at, :].astype(BF16)
-        k = K[at, :]
-        for n in range(heads):
-            g = G[at, n * kcols:(n + 1) * kcols]
-            dweight = dot(g, v, ((1,), (1,)))
-            delta = jnp.sum(P[i * heads + n].astype(F32) * dweight, axis=-1, keepdims=True)
-            dscore = (C[i * heads + n] * (dweight - delta)).astype(BF16)
-            DQ[at, n * kcols:(n + 1) * kcols] = (dot(dscore, k) * QSCALE).astype(BF16)
-
-    q1_copies = scatter(dot(qu_own, DQ[...], ((1,), (1,))).astype(BF16), AQ, RAQ, q1_send, q1_recv)
-    RSQ.at[z][:, piece:] = dot(LQ[...], DQ[...], ((0,), (0,))).astype(BF16)
-    v3_copies = spread(shared(RSV, v2_send, v2_recv), TV, OUTV, v3_send, v3_recv)
-    for copy in q1_copies:
-        copy.wait_recv()
-    RSQ.at[z][:, 0:piece] = plane_sum(AQ, RAQ)
-    q2_copies = share(RSQ, q2_send, q2_recv)
-    q3_copies = spread(shared(RSQ, q2_send, q2_recv), TQ, OUTQ, q3_send, q3_recv)
-    gathered(OUTV, v3_send, v3_recv)
-    gathered(OUTQ, q3_send, q3_recv)
-
-    for r in (1, 2, 3):
-        for copy in w_copies[r]:
-            copy.wait_send()
-    for copy in t_copies:
-        copy.wait_send()
-    for r in range(1, PLANE):
-        g_copies[r].wait_send()
-        s_copies[r].wait_send()
+    for half in range(2):
+        for i in range(half * tiles // 2, (half + 1) * tiles // 2):
+            at = pl.ds(i * seq, seq)
+            v = accv[at, :].astype(BF16)
+            k = K[at, :]
+            for n in range(heads):
+                g = G[at, n * kcols:(n + 1) * kcols]
+                dweight = dot(g, v, ((1,), (1,)))
+                delta = jnp.sum(P[i * heads + n].astype(F32) * dweight, axis=-1, keepdims=True)
+                dscore = (C[i * heads + n] * (dweight - delta)).astype(BF16)
+                DQ[at, n * kcols:(n + 1) * kcols] = (dot(dscore, k) * QSCALE).astype(BF16)
+        send_pull(half, query_up(), DQ, PQ, RPQ, q1_send, q1_recv)
+
+    low_gradient = dot(LL[...], DQ[...], ((0,), (0,)))
+    RSB[z] = low_gradient[0:ranks, :].astype(BF16)
+    share(RSB, b_sem)
+    spread(shared(RSV, v_sem), TV, OUTV, v_sem)
+    RSA[z] = down_gradient(PQ, RPQ, q1_send, q1_recv)
+    share(RSA, a_sem)
+    spread(shared(RSB, b_sem), TB, OUTB, b_sem)
+    spread(shared(RSA, a_sem), TA, OUTA, a_sem)
+    results = ((OUTV, v_sem), (OUTB, b_sem), (OUTA, a_sem))
+    for out, sem in results:
+        spreads(out, sem).wait_recv()
+
+    at = WA.at[pl.ds(0, 3 * rows)]
+    remote(at, at, w_send.at[0], w_recv.at[1], peer(1)).wait_send()
+    at = WV.at[pl.ds(0, 3 * rows)]
+    remote(at, at, w_send.at[1], w_recv.at[0], peer(1)).wait_send()
+    at = N.at[pl.ds(0, (PLANE - 1) * tok)]
+    remote(at, at, t_send.at[0], t_recv.at[0], peer(1)).wait_send()
+    g_all_copies.wait_send()
+    s_all_copies.wait_send()
     for t in range(chain - 1):
         @pl.when(has_up(t))
         def _():
-            for i in pieces_of(t):
-                up_copy(t, i).wait_send()
-            for half in range(2):
-                vup_copy(t, half).wait_send()
+            at = WA.at[plane_rows(z - t)]
+            remote(at, at, up_send.at[t], up_recv.at[t, 0], above(z + 1)).wait_send()
+            at = WV.at[plane_rows(z - t)]
+            remote(at, at, vup_send.at[t], vup_recv.at[t, 0], above(z + 1)).wait_send()
 
         @pl.when(has_down(t))
         def _():
-            for i in pieces_of(t):
-                down_copy(t, i).wait_send()
-            for half in range(2):
-                vdown_copy(t, half).wait_send()
-    for copy in v1_copies + v2_copies + v3_copies + q1_copies + q2_copies + q3_copies:
-        copy.wait_send()
-
-
-def unpack_kernel(outq, outv, out_aq, out_bq, out_av, out_bv):
+            at = WA.at[plane_rows(z + t)]
+            remote(at, at, down_send.at[t], down_recv.at[t, 0], above(z - 1)).wait_send()
+            at = WV.at[plane_rows(z + t)]
+            remote(at, at, vdown_send.at[t], vdown_recv.at[t, 0], above(z - 1)).wait_send()
+    for half in range(2):
+        pulls(half, RPV, v1_send, v1_recv).wait_send()
+        pulls(half, RPQ, q1_send, q1_recv).wait_send()
+    for sums, sem in ((RSV, v_sem), (RSB, b_sem), (RSA, a_sem)):
+        shares(sums, sem).wait_send()
+    for out, sem in results:
+        spreads(out, sem).wait_send()
+
+
+def unpack_kernel(outa, outb, outv, out_aq, out_bq, out_av, out_bv):
     feats = out_aq.shape[1]
     piece = feats // PLANE
     qcols = out_bq.shape[1] // PLANE
     kcols = out_bv.shape[1] // PLANE
     for h in range(PLANE):
-        value = outq[h].astype(F32)
-        out_aq[:, h * piece:(h + 1) * piece] = value[:, 0:piece]
-        out_bq[:, h * qcols:(h + 1) * qcols] = value[:, piece:]
+        out_aq[:, h * piece:(h + 1) * piece] = outa[h].astype(F32)
+        out_bq[:, h * qcols:(h + 1) * qcols] = outb[h].astype(F32)
         value = outv[h].astype(F32)
         out_av[:, h * piece:(h + 1) * piece] = value[:, 0:piece]
         out_bv[:, h * kcols:(h + 1) * kcols] = value[:, piece:]
@@ -781,14 +800,15 @@
     steps = chain - 1
     tiles = many // (2 * tok)
     heads = qcols // kcols
-    outq, outv = pl.pallas_call(
+    outa, outb, outv = pl.pallas_call(
         functools.partial(plane_kernel, chain, coefficient),
         out_shape=(
-            pltpu.VMEM((PLANE, ranks, piece + qcols), BF16),
+            pltpu.VMEM((PLANE, ranks, piece), BF16),
+            pltpu.VMEM((PLANE, ranks, qcols), BF16),
             pltpu.VMEM((PLANE, ranks, piece + kcols), BF16),
         ),
-        in_specs=[hbm, hbm, vmem, hbm, hbm, hbm, vmem, vmem, vmem, vmem, hbm],
-        out_specs=(vmem, vmem),
+        in_specs=[hbm] * 11,
+        out_specs=(vmem, vmem, vmem),
         scratch_shapes=[
             pltpu.VMEM((many, feats), BF16),
             pltpu.VMEM((many, feats), BF16),
@@ -803,23 +823,26 @@
             pltpu.VMEM((many, kcols), BF16),
             pltpu.VMEM((many, qcols), BF16),
             pltpu.VMEM((many, kcols), BF16),
-            pltpu.VMEM((many, ranks), BF16),
-            pltpu.VMEM((many, ranks), BF16),
-            pltpu.VMEM((PLANE, ranks, piece), BF16),
-            pltpu.VMEM((PLANE, ranks, piece), BF16),
-            pltpu.VMEM((chain, ranks, piece + qcols), BF16),
-            pltpu.VMEM((ranks, piece + qcols), BF16),
-            pltpu.VMEM((PLANE, ranks, piece), BF16),
-            pltpu.VMEM((PLANE, ranks, piece), BF16),
+            pltpu.VMEM((many, 2 * ranks), BF16),
+            pltpu.VMEM((feats,), BF16),
+            pltpu.VMEM((2 * ranks, feats), BF16),
+            pltpu.VMEM((ranks, query_weight.shape[1]), BF16),
+            pltpu.VMEM((ranks, value_weight.shape[1]), BF16),
+            pltpu.VMEM((2, ranks, many // 2), BF16),
+            pltpu.VMEM((2, PLANE, ranks, many // 2), BF16),
+            pltpu.VMEM((2, ranks, many // 2), BF16),
+            pltpu.VMEM((2, PLANE, ranks, many // 2), BF16),
+            pltpu.VMEM((chain, ranks, piece), BF16),
+            pltpu.VMEM((chain, ranks, qcols), BF16),
             pltpu.VMEM((chain, ranks, piece + kcols), BF16),
+            pltpu.VMEM((ranks, piece), BF16),
+            pltpu.VMEM((ranks, qcols), BF16),
             pltpu.VMEM((ranks, piece + kcols), BF16),
-            dma((6,)),
-            dma((4, 3)), dma((4, 3)),
-            dma((8, 4)), dma((8, 4)), dma((8,)), dma((8,)), dma((8,)), dma((8,)),
-            dma((steps, 4)), dma((steps, 4)), dma((steps, 4)), dma((steps, 4)),
-            dma((steps, 2)), dma((steps, 2)), dma((steps, 2)), dma((steps, 2)),
-            dma((8,)), dma((8,)), dma((chain,)), dma((chain,)), dma((8,)), dma((8,)),
-            dma((8,)), dma((8,)), dma((chain,)), dma((chain,)), dma((8,)), dma((8,)),
+            dma((11,)),
+            dma((2,)), dma((4,)), dma((1,)), dma((11,)), dma((2,)), dma((2,)),
+            dma((steps,)), dma((steps, 2)), dma((steps,)), dma((steps, 2)),
+            dma((steps,)), dma((steps, 2)), dma((steps,)), dma((steps, 2)),
+            dma((2,)), dma((2,)), dma((2,)), dma((2,)), dma((4,)), dma((4,)), dma((4,)),
         ],
         compiler_params=pltpu.CompilerParams(
             collective_id=0, has_side_effects=True, vmem_limit_bytes=56 * 1024 * 1024
@@ -838,10 +861,10 @@
             jax.ShapeDtypeStruct((ranks, feats), F32),
             jax.ShapeDtypeStruct((ranks, value_weight.shape[1]), F32),
         ),
-        in_specs=[vmem, vmem],
+        in_specs=[vmem, vmem, vmem],
         out_specs=(vmem, vmem, vmem, vmem),
         compiler_params=pltpu.CompilerParams(vmem_limit_bytes=16 * 1024 * 1024),
-    )(outq, outv)
+    )(outa, outb, outv)
     return (aq.T, bq, av.T, bv)
 
 

time: 77.9 us -> 74.5 us (0.956)
  Pallas kernels: 77.1 us -> 73.7 us
    pallas_call x1, Pallas kernels: 76.3 us -> 72.9 us  [on_plane(): pl.pallas_call(functools.partial(plane_kernel, chain, coefficient), out_s...]
where the time goes in v3:
time: 74.5 us; the launch traced here: 74.4 us
  Pallas kernels  73.7 us (99%)
    pallas_call x1, Pallas kernels, on_plane(): pl.pallas_call(functools.partial(plane_kernel, chain, coefficient), out_s...  72.9 us

profile of v3, /device:TPU:0, one launch (start us, length us, event | category | flops | bytes accessed | tf_op | source)
XLA Modules:
  0.0 74.4 jit_solution(15436273145331613775)
XLA Ops:
  0.6 72.9 %shard_map.138 = (bf16[8,16,384]{2,1,0:T(8,128)(2,1)S(1)}, bf16[8,16,256]{2,1,0:T(8,128)(2,1)S(1)}, bf16[8,16,512]{2,1,0:T(8,128)(2,1)S(1)}) custom-call(bf16[128,3072]{1,0:T(8,128)(2,1)} %bitcast.6, s32[1,128]{1,0:T(1,128)} %seg.1, bf16[3072]{0:T(1024)(128)(2,1)} %gain_in.1, bf16[192,2048]{1,0:T(8,128)(2,1)} %wq.1, bf16[192,1024]{1,0:T(8,128)(2,1)} %wk.1, ...), custom_call_target="tpu_custom_call" | custom-call | tf_op jit(solution)/shard_map/pallas_call | solution.py:803
  73.5 0.8 %shard_map.139 = (f32[16,3072]{1,0:T(8,128)}, f32[16,2048]{1,0:T(8,128)}, f32[16,3072]{1,0:T(8,128)}, f32[16,1024]{1,0:T(8,128)}) custom-call(bf16[8,16,384]{2,1,0:T(8,128)(2,1)S(1)} %get-tuple-element.11.outa, bf16[8,16,256]{2,1,0:T(8,128)(2,1)S(1)} %get-tuple-element.12.outb, bf16[8,16,512]{2,1,0:T(8,128)(2,1)S(1)} %get-tuple-element.13.outv), custom_call_target="tpu_custom_call" | custom-call | tf_op jit(solution)/shard_map/pallas_call | solution.py:856

commit v4 on v3

--- a/solution.py
+++ b/solution.py
@@ -180,7 +180,7 @@
     OUTA, OUTB, OUTV,
     N, M, WA, WV, G, SG, acc, accv, P, C, K, DQ, DV, LL,
     gain, down, qu, vu,
-    PQ, RPQ, PV, RPV, RSA, RSB, RSV, TA, TB, TV,
+    PQ, PV, RSA, RSB, RSV, TA, TB, TV,
     local_sem, w_send, w_recv, t_send, t_recv, g_sem, s_sem,
     up_send, up_recv, down_send, down_recv, vup_send, vup_recv, vdown_send, vdown_recv,
     q1_send, q1_recv, v1_send, v1_recv, a_sem, b_sem, v_sem,
@@ -476,6 +476,19 @@
             at = part_at(part, i, seq)
             acc[at, :] = acc[at, :] + dot(M[at, chosen], WA[chosen, :])
 
+    def add_near(part):
+        low = jnp.maximum(z - 2, 0)
+        high = jnp.minimum(z + 2, chain - 1)
+        for count in range(3, min(chain, 5) + 1):
+            @pl.when(high - low == count - 1)
+            def _():
+                chosen = pl.ds(pl.multiple_of(low * 4 * rows, 4 * rows), count * 4 * rows)
+
+                @pl.loop(0, part_rows // seq)
+                def _(i):
+                    at = part_at(part, i, seq)
+                    acc[at, :] = acc[at, :] + dot(M[at, chosen], WA[chosen, :])
+
     def add_step(t, half, part):
         @pl.when(from_below(t))
         def _():
@@ -486,7 +499,7 @@
             add_piece(z + 1 + t, half, part)
 
     def add_value_piece(plane, half):
-        chosen = half_rows(plane, half)
+        chosen = plane_rows(plane) if half is None else half_rows(plane, half)
 
         @pl.loop(0, 2 * part_rows // seq)
         def _(i):
@@ -540,10 +553,6 @@
     prepare(5)
     recv_half(1, 0)
     send_chain(2, 0)
-    for half in range(2):
-        add_piece(z, half, 0)
-    for half in range(2):
-        add_step(0, half, 0)
     wait_token(2, 3, 1)
     send_token(2, 3, 1)
     prepare(2)
@@ -553,8 +562,7 @@
     send_chain(2, 1)
     for k in range(2, chain):
         send_value_first(k)
-    for half in range(2):
-        add_step(1, half, 0)
+    add_near(0)
     wait_token(6)
     send_token(6, 7, 1)
     prepare(6)
@@ -567,11 +575,7 @@
             recv_value(0, half)
             send_value(1, half)
 
-    for half in range(2):
-        add_piece(z, half, 1)
-    for t in range(2):
-        for half in range(2):
-            add_step(t, half, 1)
+    add_near(1)
     for t in range(2, chain - 1):
         for half in range(2):
             recv_half(t, half)
@@ -632,25 +636,24 @@
     def token_half(half):
         return pl.ds(half * half_tokens, half_tokens)
 
-    def send_pull(half, up, change, mine, arrived, send, recv):
-        mine[half] = dot(up, change[token_half(half), :], ((1,), (1,))).astype(BF16)
+    def send_pull(half, up, change, gathered, send, recv):
+        own = gathered.at[half, h]
+        own[...] = dot(up, change[token_half(half), :], ((1,), (1,))).astype(BF16)
         for r in (7, 6, 5, 4, 3, 2, 1):
-            remote(mine.at[half], arrived.at[half, r], send.at[half], recv.at[half], peer(r)).start()
-
-    def pulls(half, arrived, send, recv):
-        at = arrived.at[half, pl.ds(1, PLANE - 1)]
+            remote(own, own, send.at[half], recv.at[half], peer(r)).start()
+
+    def pulls(half, gathered, send, recv):
+        at = gathered.at[half, pl.ds(0, PLANE - 1)]
         return remote(at, at, send.at[half], recv.at[half], peer(1))
 
-    own_columns = pl.ds(pl.multiple_of(h * piece, piece), piece)
-
-    def down_gradient(mine, arrived, send, recv):
-        total = jnp.zeros((ranks, piece), F32)
+    def down_gradient(columns, width, gathered, send, recv):
+        total = jnp.zeros((ranks, width), F32)
         for half in range(2):
-            pulls(half, arrived, send, recv).wait_recv()
-            pull = mine[half].astype(F32)
+            pulls(half, gathered, send, recv).wait_recv()
+            pull = gathered[half, 0].astype(F32)
             for r in range(1, PLANE):
-                pull = pull + arrived[half, r].astype(F32)
-            total = total + dot(pull.astype(BF16), M[token_half(half), own_columns])
+                pull = pull + gathered[half, r].astype(F32)
+            total = total + dot(pull.astype(BF16), M[token_half(half), columns])
         return total.astype(BF16)
 
     def share(sums, sem):
@@ -680,19 +683,19 @@
         return remote(at, at, sem.at[2], sem.at[3], peer(1))
 
     for half in range(2):
-        send_pull(half, value_up(), DV, PV, RPV, v1_send, v1_recv)
+        send_pull(half, value_up(), DV, PV, v1_send, v1_recv)
     low_gradient = dot(LL[...], DV[...], ((0,), (0,)))
     RSV.at[z][:, piece:] = low_gradient[ranks:, :].astype(BF16)
-    for half in range(2):
-        add_value_piece(z, half)
+    add_value_piece(z, None)
     for t in range(chain - 2):
-        for half in range(2):
-            @pl.when(outer)
-            def _():
+        @pl.when(outer)
+        def _():
+            for half in range(2):
                 recv_value(t, half)
 
-            add_value(t, half)
-    RSV.at[z][:, 0:piece] = down_gradient(PV, RPV, v1_send, v1_recv)
+        add_value(t, None)
+    own_columns = pl.ds(pl.multiple_of(h * piece, piece), piece)
+    RSV.at[z][:, 0:piece] = down_gradient(own_columns, piece, PV, v1_send, v1_recv)
     share(RSV, v_sem)
     for half in range(2):
         @pl.when(outer)
@@ -712,19 +715,26 @@
                 delta = jnp.sum(P[i * heads + n].astype(F32) * dweight, axis=-1, keepdims=True)
                 dscore = (C[i * heads + n] * (dweight - delta)).astype(BF16)
                 DQ[at, n * kcols:(n + 1) * kcols] = (dot(dscore, k) * QSCALE).astype(BF16)
-        send_pull(half, query_up(), DQ, PQ, RPQ, q1_send, q1_recv)
+        send_pull(half, query_up(), DQ, PQ, q1_send, q1_recv)
 
     low_gradient = dot(LL[...], DQ[...], ((0,), (0,)))
     RSB[z] = low_gradient[0:ranks, :].astype(BF16)
     share(RSB, b_sem)
     spread(shared(RSV, v_sem), TV, OUTV, v_sem)
-    RSA[z] = down_gradient(PQ, RPQ, q1_send, q1_recv)
+    width = feats // 2
+    core_columns = pl.ds(pl.multiple_of(c * width, width), width)
+    RSA[z] = down_gradient(core_columns, width, PQ, q1_send, q1_recv)
     share(RSA, a_sem)
     spread(shared(RSB, b_sem), TB, OUTB, b_sem)
-    spread(shared(RSA, a_sem), TA, OUTA, a_sem)
-    results = ((OUTV, v_sem), (OUTB, b_sem), (OUTA, a_sem))
+    TA[...] = shared(RSA, a_sem)
+    core_copy = remote(TA, OUTA.at[c], a_sem.at[2], a_sem.at[3], peer(1))
+    core_copy.start()
+    OUTA[c] = TA[...]
+    results = ((OUTV, v_sem), (OUTB, b_sem))
     for out, sem in results:
         spreads(out, sem).wait_recv()
+    at = OUTA.at[1 - c]
+    remote(at, at, a_sem.at[2], a_sem.at[3], peer(1)).wait_recv()
 
     at = WA.at[pl.ds(0, 3 * rows)]
     remote(at, at, w_send.at[0], w_recv.at[1], peer(1)).wait_send()
@@ -749,12 +759,13 @@
             at = WV.at[plane_rows(z + t)]
             remote(at, at, vdown_send.at[t], vdown_recv.at[t, 0], above(z - 1)).wait_send()
     for half in range(2):
-        pulls(half, RPV, v1_send, v1_recv).wait_send()
-        pulls(half, RPQ, q1_send, q1_recv).wait_send()
+        pulls(half, PV, v1_send, v1_recv).wait_send()
+        pulls(half, PQ, q1_send, q1_recv).wait_send()
     for sums, sem in ((RSV, v_sem), (RSB, b_sem), (RSA, a_sem)):
         shares(sums, sem).wait_send()
     for out, sem in results:
         spreads(out, sem).wait_send()
+    core_copy.wait_send()
 
 
 def unpack_kernel(outa, outb, outv, out_aq, out_bq, out_av, out_bv):
@@ -762,8 +773,9 @@
     piece = feats // PLANE
     qcols = out_bq.shape[1] // PLANE
     kcols = out_bv.shape[1] // PLANE
+    for core in range(2):
+        out_aq[:, core * feats // 2:(core + 1) * feats // 2] = outa[core].astype(F32)
     for h in range(PLANE):
-        out_aq[:, h * piece:(h + 1) * piece] = outa[h].astype(F32)
         out_bq[:, h * qcols:(h + 1) * qcols] = outb[h].astype(F32)
         value = outv[h].astype(F32)
         out_av[:, h * piece:(h + 1) * piece] = value[:, 0:piece]
@@ -803,7 +815,7 @@
     outa, outb, outv = pl.pallas_call(
         functools.partial(plane_kernel, chain, coefficient),
         out_shape=(
-            pltpu.VMEM((PLANE, ranks, piece), BF16),
+            pltpu.VMEM((2, ranks, feats // 2), BF16),
             pltpu.VMEM((PLANE, ranks, qcols), BF16),
             pltpu.VMEM((PLANE, ranks, piece + kcols), BF16),
         ),
@@ -828,14 +840,12 @@
             pltpu.VMEM((2 * ranks, feats), BF16),
             pltpu.VMEM((ranks, query_weight.shape[1]), BF16),
             pltpu.VMEM((ranks, value_weight.shape[1]), BF16),
-            pltpu.VMEM((2, ranks, many // 2), BF16),
             pltpu.VMEM((2, PLANE, ranks, many // 2), BF16),
-            pltpu.VMEM((2, ranks, many // 2), BF16),
             pltpu.VMEM((2, PLANE, ranks, many // 2), BF16),
-            pltpu.VMEM((chain, ranks, piece), BF16),
+            pltpu.VMEM((chain, ranks, feats // 2), BF16),
             pltpu.VMEM((chain, ranks, qcols), BF16),
             pltpu.VMEM((chain, ranks, piece + kcols), BF16),
-            pltpu.VMEM((ranks, piece), BF16),
+            pltpu.VMEM((ranks, feats // 2), BF16),
             pltpu.VMEM((ranks, qcols), BF16),
             pltpu.VMEM((ranks, piece + kcols), BF16),
             dma((11,)),

time: 74.5 us -> 73.3 us (0.984)
  Pallas kernels: 73.7 us -> 72.5 us
    pallas_call x1, Pallas kernels: 72.9 us -> 71.7 us  [on_plane(): pl.pallas_call(functools.partial(plane_kernel, chain, coefficient), out_s...]
where the time goes in v4:
time: 73.3 us; the launch traced here: 73.1 us
  Pallas kernels  72.5 us (99%)
    pallas_call x1, Pallas kernels, on_plane(): pl.pallas_call(functools.partial(plane_kernel, chain, coefficient), out_s...  71.7 us

profile of v4, /device:TPU:0, one launch (start us, length us, event | category | flops | bytes accessed | tf_op | source)
XLA Modules:
  0.0 73.1 jit_solution(16007094360280398159)
XLA Ops:
  0.6 71.7 %shard_map.138 = (bf16[2,16,1536]{2,1,0:T(8,128)(2,1)S(1)}, bf16[8,16,256]{2,1,0:T(8,128)(2,1)S(1)}, bf16[8,16,512]{2,1,0:T(8,128)(2,1)S(1)}) custom-call(bf16[128,3072]{1,0:T(8,128)(2,1)} %bitcast.6, s32[1,128]{1,0:T(1,128)} %seg.1, bf16[3072]{0:T(1024)(128)(2,1)} %gain_in.1, bf16[192,2048]{1,0:T(8,128)(2,1)} %wq.1, bf16[192,1024]{1,0:T(8,128)(2,1)} %wk.1, ...), custom_call_target="tpu_custom_call" | custom-call | tf_op jit(solution)/shard_map/pallas_call | solution.py:815
  72.3 0.8 %shard_map.139 = (f32[16,3072]{1,0:T(8,128)}, f32[16,2048]{1,0:T(8,128)}, f32[16,3072]{1,0:T(8,128)}, f32[16,1024]{1,0:T(8,128)}) custom-call(bf16[2,16,1536]{2,1,0:T(8,128)(2,1)S(1)} %get-tuple-element.11.outa, bf16[8,16,256]{2,1,0:T(8,128)(2,1)S(1)} %get-tuple-element.12.outb, bf16[8,16,512]{2,1,0:T(8,128)(2,1)S(1)} %get-tuple-element.13.outv), custom_call_target="tpu_custom_call" | custom-call | tf_op jit(solution)/shard_map/pallas_call | solution.py:866

commit v5 on v4

--- a/solution.py
+++ b/solution.py
@@ -177,13 +177,13 @@
 def plane_kernel(
     chain, coefficient,
     raw, seg, gain_in, wq, wk, wv, qd, qu_in, vd, vu_in, grad,
-    OUTA, OUTB, OUTV,
+    OUTA, OUTV,
     N, M, WA, WV, G, SG, acc, accv, P, C, K, DQ, DV, LL,
     gain, down, qu, vu,
-    PQ, PV, RSA, RSB, RSV, TA, TB, TV,
+    PQ, PV, RSA, RSV, TA, TV,
     local_sem, w_send, w_recv, t_send, t_recv, g_sem, s_sem,
     up_send, up_recv, down_send, down_recv, vup_send, vup_recv, vdown_send, vdown_recv,
-    q1_send, q1_recv, v1_send, v1_recv, a_sem, b_sem, v_sem,
+    q1_send, q1_recv, v1_send, v1_recv, a_sem, v_sem,
 ):
     x = lax.axis_index("ctx")
     f = lax.axis_index("fsdp")
@@ -665,8 +665,7 @@
         at = sums.at[pl.ds(0, chain - 1)]
         return remote(at, at, sem.at[0], sem.at[1], peer(1))
 
-    def shared(sums, sem):
-        shares(sums, sem).wait_recv()
+    def shared(sums):
         total = sums[0].astype(F32)
         for d in range(1, chain):
             total = total + sums[d].astype(F32)
@@ -685,7 +684,7 @@
     for half in range(2):
         send_pull(half, value_up(), DV, PV, v1_send, v1_recv)
     low_gradient = dot(LL[...], DV[...], ((0,), (0,)))
-    RSV.at[z][:, piece:] = low_gradient[ranks:, :].astype(BF16)
+    RSV.at[z][:, piece:piece + kcols] = low_gradient[ranks:, :].astype(BF16)
     add_value_piece(z, None)
     for t in range(chain - 2):
         @pl.when(outer)
@@ -696,7 +695,6 @@
         add_value(t, None)
     own_columns = pl.ds(pl.multiple_of(h * piece, piece), piece)
     RSV.at[z][:, 0:piece] = down_gradient(own_columns, piece, PV, v1_send, v1_recv)
-    share(RSV, v_sem)
     for half in range(2):
         @pl.when(outer)
         def _():
@@ -718,21 +716,29 @@
         send_pull(half, query_up(), DQ, PQ, q1_send, q1_recv)
 
     low_gradient = dot(LL[...], DQ[...], ((0,), (0,)))
-    RSB[z] = low_gradient[0:ranks, :].astype(BF16)
-    share(RSB, b_sem)
-    spread(shared(RSV, v_sem), TV, OUTV, v_sem)
+    RSV.at[z][:, piece + kcols:] = low_gradient[0:ranks, :].astype(BF16)
+    share(RSV, v_sem)
     width = feats // 2
     core_columns = pl.ds(pl.multiple_of(c * width, width), width)
     RSA[z] = down_gradient(core_columns, width, PQ, q1_send, q1_recv)
-    share(RSA, a_sem)
-    spread(shared(RSB, b_sem), TB, OUTB, b_sem)
-    TA[...] = shared(RSA, a_sem)
+
+    @pl.when(outer)
+    def _():
+        share(RSA, a_sem)
+
+    shares(RSV, v_sem).wait_recv()
+
+    @pl.when(middle)
+    def _():
+        share(RSA, a_sem)
+
+    spread(shared(RSV), TV, OUTV, v_sem)
+    shares(RSA, a_sem).wait_recv()
+    TA[...] = shared(RSA)
     core_copy = remote(TA, OUTA.at[c], a_sem.at[2], a_sem.at[3], peer(1))
     core_copy.start()
     OUTA[c] = TA[...]
-    results = ((OUTV, v_sem), (OUTB, b_sem))
-    for out, sem in results:
-        spreads(out, sem).wait_recv()
+    spreads(OUTV, v_sem).wait_recv()
     at = OUTA.at[1 - c]
     remote(at, at, a_sem.at[2], a_sem.at[3], peer(1)).wait_recv()
 
@@ -761,14 +767,13 @@
     for half in range(2):
         pulls(half, PV, v1_send, v1_recv).wait_send()
         pulls(half, PQ, q1_send, q1_recv).wait_send()
-    for sums, sem in ((RSV, v_sem), (RSB, b_sem), (RSA, a_sem)):
+    for sums, sem in ((RSV, v_sem), (RSA, a_sem)):
         shares(sums, sem).wait_send()
-    for out, sem in results:
-        spreads(out, sem).wait_send()
+    spreads(OUTV, v_sem).wait_send()
     core_copy.wait_send()
 
 
-def unpack_kernel(outa, outb, outv, out_aq, out_bq, out_av, out_bv):
+def unpack_kernel(outa, outv, out_aq, out_bq, out_av, out_bv):
     feats = out_aq.shape[1]
     piece = feats // PLANE
     qcols = out_bq.shape[1] // PLANE
@@ -776,10 +781,10 @@
     for core in range(2):
         out_aq[:, core * feats // 2:(core + 1) * feats // 2] = outa[core].astype(F32)
     for h in range(PLANE):
-        out_bq[:, h * qcols:(h + 1) * qcols] = outb[h].astype(F32)
         value = outv[h].astype(F32)
+        out_bq[:, h * qcols:(h + 1) * qcols] = value[:, piece + kcols:]
         out_av[:, h * piece:(h + 1) * piece] = value[:, 0:piece]
-        out_bv[:, h * kcols:(h + 1) * kcols] = value[:, piece:]
+        out_bv[:, h * kcols:(h + 1) * kcols] = value[:, piece:piece + kcols]
 
 
 def on_plane(
@@ -812,15 +817,14 @@
     steps = chain - 1
     tiles = many // (2 * tok)
     heads = qcols // kcols
-    outa, outb, outv = pl.pallas_call(
+    outa, outv = pl.pallas_call(
         functools.partial(plane_kernel, chain, coefficient),
         out_shape=(
             pltpu.VMEM((2, ranks, feats // 2), BF16),
-            pltpu.VMEM((PLANE, ranks, qcols), BF16),
-            pltpu.VMEM((PLANE, ranks, piece + kcols), BF16),
+            pltpu.VMEM((PLANE, ranks, piece + kcols + qcols), BF16),
         ),
         in_specs=[hbm] * 11,
-        out_specs=(vmem, vmem, vmem),
+        out_specs=(vmem, vmem),
         scratch_shapes=[
             pltpu.VMEM((many, feats), BF16),
             pltpu.VMEM((many, feats), BF16),
@@ -843,16 +847,14 @@
             pltpu.VMEM((2, PLANE, ranks, many // 2), BF16),
             pltpu.VMEM((2, PLANE, ranks, many // 2), BF16),
             pltpu.VMEM((chain, ranks, feats // 2), BF16),
-            pltpu.VMEM((chain, ranks, qcols), BF16),
-            pltpu.VMEM((chain, ranks, piece + kcols), BF16),
+            pltpu.VMEM((chain, ranks, piece + kcols + qcols), BF16),
             pltpu.VMEM((ranks, feats // 2), BF16),
-            pltpu.VMEM((ranks, qcols), BF16),
-            pltpu.VMEM((ranks, piece + kcols), BF16),
+            pltpu.VMEM((ranks, piece + kcols + qcols), BF16),
             dma((11,)),
             dma((2,)), dma((4,)), dma((1,)), dma((11,)), dma((2,)), dma((2,)),
             dma((steps,)), dma((steps, 2)), dma((steps,)), dma((steps, 2)),
             dma((steps,)), dma((steps, 2)), dma((steps,)), dma((steps, 2)),
-            dma((2,)), dma((2,)), dma((2,)), dma((2,)), dma((4,)), dma((4,)), dma((4,)),
+            dma((2,)), dma((2,)), dma((2,)), dma((2,)), dma((4,)), dma((4,)),
         ],
         compiler_params=pltpu.CompilerParams(
             collective_id=0, has_side_effects=True, vmem_limit_bytes=56 * 1024 * 1024
@@ -871,10 +873,10 @@
             jax.ShapeDtypeStruct((ranks, feats), F32),
             jax.ShapeDtypeStruct((ranks, value_weight.shape[1]), F32),
         ),
-        in_specs=[vmem, vmem, vmem],
+        in_specs=[vmem, vmem],
         out_specs=(vmem, vmem, vmem, vmem),
         compiler_params=pltpu.CompilerParams(vmem_limit_bytes=16 * 1024 * 1024),
-    )(outa, outb, outv)
+    )(outa, outv)
     return (aq.T, bq, av.T, bv)
 
 

time: 73.3 us -> 72.4 us (0.988)
  Pallas kernels: 72.5 us -> 71.6 us
    pallas_call x1, Pallas kernels: 71.7 us -> 70.8 us  [on_plane(): pl.pallas_call(functools.partial(plane_kernel, chain, coefficient), out_s...]
where the time goes in v5:
time: 72.4 us; the launch traced here: 72.3 us
  Pallas kernels  71.6 us (99%)
    pallas_call x1, Pallas kernels, on_plane(): pl.pallas_call(functools.partial(plane_kernel, chain, coefficient), out_s...  70.8 us

profile of v5, /device:TPU:0, one launch (start us, length us, event | category | flops | bytes accessed | tf_op | source)
XLA Modules:
  0.0 72.3 jit_solution(15459872611412945035)
XLA Ops:
  0.6 70.8 %shard_map.138 = (bf16[2,16,1536]{2,1,0:T(8,128)(2,1)S(1)}, bf16[8,16,768]{2,1,0:T(8,128)(2,1)S(1)}) custom-call(bf16[128,3072]{1,0:T(8,128)(2,1)} %bitcast.6, s32[1,128]{1,0:T(1,128)} %seg.1, bf16[3072]{0:T(1024)(128)(2,1)} %gain_in.1, bf16[192,2048]{1,0:T(8,128)(2,1)} %wq.1, bf16[192,1024]{1,0:T(8,128)(2,1)} %wk.1, bf16[192,1024]{1,0:T(8,128)(2,1)} %wv.1, ...), custom_call_target="tpu_custom_call" | custom-call | tf_op jit(solution)/shard_map/pallas_call | solution.py:820
  71.4 0.8 %shard_map.139 = (f32[16,3072]{1,0:T(8,128)}, f32[16,2048]{1,0:T(8,128)}, f32[16,3072]{1,0:T(8,128)}, f32[16,1024]{1,0:T(8,128)}) custom-call(bf16[2,16,1536]{2,1,0:T(8,128)(2,1)S(1)} %get-tuple-element.10.outa, bf16[8,16,768]{2,1,0:T(8,128)(2,1)S(1)} %get-tuple-element.11.outv), custom_call_target="tpu_custom_call" | custom-call | tf_op jit(solution)/shard_map/pallas_call | solution.py:868

commit v6 on v5

--- a/solution.py
+++ b/solution.py
@@ -394,10 +394,10 @@
             remote(a, b, w_send.at[i // 2], w_recv.at[r if i < 2 else 0], peer(r))
             for i, (a, b) in enumerate(w_parts(r))
         ]
+    send_chain(0, 0)
     for r in (1, 2, 3):
         for i in range(2):
             w_copies[r][i].start()
-    send_chain(0, 0)
     for r in (1, 2, 3):
         w_copies[r][2].start()
 
@@ -576,6 +576,7 @@
             send_value(1, half)
 
     add_near(1)
+    add_value_piece(z, None)
     for t in range(2, chain - 1):
         for half in range(2):
             recv_half(t, half)
@@ -685,7 +686,6 @@
         send_pull(half, value_up(), DV, PV, v1_send, v1_recv)
     low_gradient = dot(LL[...], DV[...], ((0,), (0,)))
     RSV.at[z][:, piece:piece + kcols] = low_gradient[ranks:, :].astype(BF16)
-    add_value_piece(z, None)
     for t in range(chain - 2):
         @pl.when(outer)
         def _():
@@ -721,17 +721,8 @@
     width = feats // 2
     core_columns = pl.ds(pl.multiple_of(c * width, width), width)
     RSA[z] = down_gradient(core_columns, width, PQ, q1_send, q1_recv)
-
-    @pl.when(outer)
-    def _():
-        share(RSA, a_sem)
-
+    share(RSA, a_sem)
     shares(RSV, v_sem).wait_recv()
-
-    @pl.when(middle)
-    def _():
-        share(RSA, a_sem)
-
     spread(shared(RSV), TV, OUTV, v_sem)
     shares(RSA, a_sem).wait_recv()
     TA[...] = shared(RSA)

time: 72.4 us -> 72.2 us (level)
  no operation moved by 1% of the time
where the time goes in v6:
time: 72.2 us; the launch traced here: 72 us
  Pallas kernels  71.4 us (99%)
    pallas_call x1, Pallas kernels, on_plane(): pl.pallas_call(functools.partial(plane_kernel, chain, coefficient), out_s...  70.6 us

profile of v6, /device:TPU:0, one launch (start us, length us, event | category | flops | bytes accessed | tf_op | source)
XLA Modules:
  0.0 72.0 jit_solution(1421066640907015682)
XLA Ops:
  0.6 70.6 %shard_map.138 = (bf16[2,16,1536]{2,1,0:T(8,128)(2,1)S(1)}, bf16[8,16,768]{2,1,0:T(8,128)(2,1)S(1)}) custom-call(bf16[128,3072]{1,0:T(8,128)(2,1)} %bitcast.6, s32[1,128]{1,0:T(1,128)} %seg.1, bf16[3072]{0:T(1024)(128)(2,1)} %gain_in.1, bf16[192,2048]{1,0:T(8,128)(2,1)} %wq.1, bf16[192,1024]{1,0:T(8,128)(2,1)} %wk.1, bf16[192,1024]{1,0:T(8,128)(2,1)} %wv.1, ...), custom_call_target="tpu_custom_call" | custom-call | tf_op jit(solution)/shard_map/pallas_call | solution.py:811
  71.2 0.8 %shard_map.139 = (f32[16,3072]{1,0:T(8,128)}, f32[16,2048]{1,0:T(8,128)}, f32[16,3072]{1,0:T(8,128)}, f32[16,1024]{1,0:T(8,128)}) custom-call(bf16[2,16,1536]{2,1,0:T(8,128)(2,1)S(1)} %get-tuple-element.10.outa, bf16[8,16,768]{2,1,0:T(8,128)(2,1)S(1)} %get-tuple-element.11.outv), custom_call_target="tpu_custom_call" | custom-call | tf_op jit(solution)/shard_map/pallas_call | solution.py:859

commit v7 on v6

--- a/solution.py
+++ b/solution.py
@@ -659,8 +659,9 @@
 
     def share(sums, sem):
         own = sums.at[z]
+        turn = jnp.where(2 * z < chain, chain - 1, 1)
         for d in range(1, chain):
-            remote(own, own, sem.at[0], sem.at[1], above((z + d) % chain)).start()
+            remote(own, own, sem.at[0], sem.at[1], above((z + turn * d) % chain)).start()
 
     def shares(sums, sem):
         at = sums.at[pl.ds(0, chain - 1)]

time: 72.2 us -> 72.1 us (level)
  no operation moved by 1% of the time
where the time goes in v7:
time: 72.1 us; the launch traced here: 72 us
  Pallas kernels  71.4 us (99%)
    pallas_call x1, Pallas kernels, on_plane(): pl.pallas_call(functools.partial(plane_kernel, chain, coefficient), out_s...  70.5 us

profile of v7, /device:TPU:0, one launch (start us, length us, event | category | flops | bytes accessed | tf_op | source)
XLA Modules:
  0.0 72.0 jit_solution(14158399446707488715)
XLA Ops:
  0.6 70.5 %shard_map.138 = (bf16[2,16,1536]{2,1,0:T(8,128)(2,1)S(1)}, bf16[8,16,768]{2,1,0:T(8,128)(2,1)S(1)}) custom-call(bf16[128,3072]{1,0:T(8,128)(2,1)} %bitcast.6, s32[1,128]{1,0:T(1,128)} %seg.1, bf16[3072]{0:T(1024)(128)(2,1)} %gain_in.1, bf16[192,2048]{1,0:T(8,128)(2,1)} %wq.1, bf16[192,1024]{1,0:T(8,128)(2,1)} %wk.1, bf16[192,1024]{1,0:T(8,128)(2,1)} %wv.1, ...), custom_call_target="tpu_custom_call" | custom-call | tf_op jit(solution)/shard_map/pallas_call | solution.py:812
  71.2 0.8 %shard_map.139 = (f32[16,3072]{1,0:T(8,128)}, f32[16,2048]{1,0:T(8,128)}, f32[16,3072]{1,0:T(8,128)}, f32[16,1024]{1,0:T(8,128)}) custom-call(bf16[2,16,1536]{2,1,0:T(8,128)(2,1)S(1)} %get-tuple-element.10.outa, bf16[8,16,768]{2,1,0:T(8,128)(2,1)S(1)} %get-tuple-element.11.outv), custom_call_target="tpu_custom_call" | custom-call | tf_op jit(solution)/shard_map/pallas_call | solution.py:860
